TPU v7x, 128 devices: a whole 4x4x4 slice. The times are simulated.
128 devices in a mesh: grp: 4 (over x_hi, core), sub: 32 (over x_lo, y, z).
Axes of the slice: x: 4 (x_hi: 2, x_lo: 2; x = x_hi * 2 + x_lo), y: 4, z: 4, core: 2. Of those that a mesh axis runs over, the one named last changes fastest.
Arguments:
- template: bfloat16 [96, 96, 128], P('sub'), may hold values from -4 to 4
- subjects: bfloat16 [128, 96, 96, 128], P(('grp', 'sub')), may hold values from -40 to 40
Outputs:
- velocity: float32 [96, 3, 96, 128], P('sub')
- new_template: float32 [96, 96, 128], P('sub')
- similarity: float32 [], replicated
All inputs are finite; a program needn't handle non-finite values.
Results may differ from a plain program's by a relative error of at most 0.0003.
Values may be sent and summed in bfloat16 or wider, within the bound.
No kernel may reach another device: no remote copies, remote signals or barrier semaphores. Data moves between devices by JAX's collectives and lax.ppermute only.
A program may use at most 128 MiB of HBM per device.

v0:
```python
import functools
import math

import jax
import jax.numpy as jnp
from jax import lax
from jax.experimental import pallas as pl
from jax.experimental.pallas import tpu as pltpu
from jax.sharding import PartitionSpec as P


RADIUS = 4
REACH = 5
EPSILON = 1e-05
STEP_LENGTH = 0.5
VARIANCE = 3.0
F32 = jnp.float32
BF16 = jnp.bfloat16

NZ, NX, NY = 96, 96, 128
WIN = 56
OWN = 48
COUNT = 729.0
BOTH = ("grp", "sub")
DEVICES = 128


def place(xh, co, xl, y, z):
    return (xh * 2 + co) * 32 + xl * 16 + y * 4 + z


def pairs(move):
    out = []
    for xh in range(2):
        for co in range(2):
            for xl in range(2):
                for y in range(4):
                    for z in range(4):
                        target = move(xh, co, xl, y, z)
                        if target is not None:
                            out.append((place(xh, co, xl, y, z), place(*target)))
    return out


def first_round(k):
    return pairs(
        lambda xh, co, xl, y, z: (xh, co, xl, y, (z + k) % 4) if co == 0 else (xh, co, xl, (y + k) % 4, z)
    )


def second_round(k):
    return pairs(
        lambda xh, co, xl, y, z: (xh, co, xl, (y + k) % 4, z) if co == 0 else (xh, co, xl, y, (z + k) % 4)
    )


def third_round(k):
    def move(xh, co, xl, y, z):
        x = (xh * 2 + xl + k) % 4
        return (x // 2, co, x % 2, y, z)

    return pairs(move)


TWIN_PAIRS = pairs(lambda xh, co, xl, y, z: (1 - xh, co, xl, y, z))
CORE_PAIRS = pairs(lambda xh, co, xl, y, z: (xh, 1 - co, xl, y, z))


def slab_shift(k):
    return [
        (g * 32 + s, g * 32 + (s + (k if g < 2 else -k)) % 32) for g in range(4) for s in range(32)
    ]


def permute(x, table):
    return lax.ppermute(x, BOTH, table)


def slab_of(idx, kb, ka, kl):
    b = (idx[1] + kb) & 3
    a = (idx[2] + ka) & 3
    xl = (idx[3] + kl) & 1
    core = idx[0]
    y = jnp.where(core == 0, a, b)
    z = jnp.where(core == 0, b, a)
    return xl * 16 + y * 4 + z


TOP = 16
CHUNK = 4
STEPS = NZ // (2 * CHUNK)
PAGES = NZ + 2 * CHUNK
FIRST_ORDER = 1.0 / 27.0


def split(product):
    high = product.astype(BF16)
    low = (product - high.astype(F32)).astype(BF16)
    return jnp.concatenate([high, low], axis=1)


def bands():
    rows = lax.broadcasted_iota(jnp.int32, (2 * NY, NY), 0)
    cols = lax.broadcasted_iota(jnp.int32, (2 * NY, NY), 1)
    away = jnp.abs((rows & (NY - 1)) - cols)
    band2 = jnp.where(away <= RADIUS, 1.0, 0.0).astype(BF16)
    return band2[:NY], band2


def dot(lhs, rhs):
    return jnp.dot(lhs, rhs, preferred_element_type=F32)


def load(ref, base, chunk):
    return ref[pl.ds(base, chunk)].reshape(chunk * WIN, NY)


def triple_sums(makers, scales, shift, even, odd, three, last, enter, emit, leave):
    band1, band2 = bands()
    volumes = len(three)
    first = [v for v in range(volumes) if scales[v] is not None]
    second = [v for v in range(volumes) if scales[v] is None]
    for v in range(volumes):
        for ref in (even[v], odd[v], last[v]):
            ref[...] = jnp.zeros(ref.shape, F32)

    def along_y(lhs, line):
        size = CHUNK * WIN
        for members, band in ((first, band1), (second, band2)):
            sums = dot(jnp.concatenate([lhs[v]() for v in members], axis=0), band)
            for m, v in enumerate(members):
                for j in range(CHUNK):
                    at = m * size + j * WIN
                    line[v][j, pl.ds(TOP, WIN), :] = sums[at : at + WIN]

    def triples(v, n, q, rows, pages):
        before, here = last[v][0, rows, :], last[v][1, rows, :]
        left, right = here + pages[0], pages[1] + pages[2]
        sums = (before + left, left + pages[1], pages[0] + right, right + pages[3])
        for j in range(CHUNK):
            emit(v, n, q + j, rows, sums[j] * scales[v] if scales[v] is not None else sums[j])
        last[v][0, rows, :] = pages[2]
        last[v][1, rows, :] = pages[3]

    def along_x(v, line, n, q):
        for j in range(CHUNK):
            three[v][j] = (
                line[v][j, pl.ds(TOP - 9 + shift, 64), :]
                + line[v][j, pl.ds(TOP - 8 + shift, 64), :]
                + line[v][j, pl.ds(TOP - 7 + shift, 64), :]
            )
        for r in range(OWN // 8):
            pages = [
                three[v][j, pl.ds(5 + 8 * r, 8), :]
                + three[v][j, pl.ds(8 + 8 * r, 8), :]
                + three[v][j, pl.ds(11 + 8 * r, 8), :]
                for j in range(CHUNK)
            ]
            triples(v, n, q, pl.ds(8 * r, 8), pages)

    def step(n, carry):
        enter(n)
        along_y(makers(2 * n * CHUNK), even)
        for v in range(volumes):
            along_x(v, odd, n, 0)
        along_y(makers((2 * n + 1) * CHUNK), odd)
        for v in range(volumes):
            along_x(v, even, n, CHUNK)
        leave(n)
        return carry

    lax.fori_loop(0, STEPS, step, 0)
    n = jnp.int32(STEPS)
    enter(n)
    zeros = jnp.zeros((8, NY), F32)
    for v in range(volumes):
        along_x(v, odd, n, 0)
        for r in range(OWN // 8):
            triples(v, n, CHUNK, pl.ds(8 * r, 8), [zeros] * CHUNK)
    leave(n)


PARTS = 4
PART = NZ // PARTS


def window_fetches(core, pairs_of_refs, sems):
    rows = pl.ds(pl.multiple_of(core * (NX - WIN), 8), WIN)
    return [
        [
            pltpu.make_async_copy(
                ref.at[pl.ds(p * PART, PART), rows], held.at[pl.ds(p * PART, PART)], sems.at[i, p]
            )
            for i, (ref, held) in enumerate(pairs_of_refs)
        ]
        for p in range(PARTS)
    ]


def wait_part(fetches, n):
    for p in range(PARTS):

        @pl.when(n == p * (STEPS // PARTS))
        def _():
            for fetch in fetches[p]:
                fetch.wait()


def in_hbm(x):
    return pltpu.with_memory_space_constraint(x, pltpu.HBM)


def moving_kernel(
    idx, ja_hbm, jb_hbm, plane_hbm, o0, o1, o2, o3,
    ja_ref, jb_ref, pair, even, odd, three, last, ready, in_sem, pair_sem, sem,
):
    shift = pl.multiple_of(idx[0] * 8, 8)
    length = 2 * CHUNK
    fetches = window_fetches(idx[0], ((ja_hbm, ja_ref), (jb_hbm, jb_ref)), in_sem)
    for part in fetches:
        for fetch in part:
            fetch.start()

    def makers(base):
        def square(ref):
            f = load(ref, base, CHUNK).astype(F32)
            return split(f * f)

        def add():
            fa = load(ja_ref, base, CHUNK).astype(F32)
            fb = load(jb_ref, base, CHUNK).astype(F32)
            pair[pl.ds(base, CHUNK)] = (fa + fb).reshape(CHUNK, WIN, NY)
            return load(ja_ref, base, CHUNK)

        return [
            add,
            lambda: square(ja_ref),
            lambda: load(jb_ref, base, CHUNK),
            lambda: square(jb_ref),
        ]

    def copy(n):
        slot = n & (SLOTS - 1)
        return pltpu.make_async_copy(
            ready.at[slot], plane_hbm.at[:, pl.ds(n * length, length)], sem.at[slot]
        )

    outs = []
    for kb, out in enumerate((o0, o1, o2, o3)):
        for t in range(8):
            slab = slab_of(idx, kb, t // 2, t % 2)
            outs.append(
                pltpu.make_async_copy(
                    pair.at[pl.ds(slab * 3, 3), pl.ds(shift, OWN)], out.at[t], pair_sem.at[kb * 8 + t]
                )
            )

    def enter(n):
        wait_part(fetches, n)

        @pl.when(n >= SLOTS)
        def _():
            copy(n - SLOTS).wait()

        @pl.when(n == STEPS)
        def _():
            for out in outs:
                out.start()

    def emit(v, n, q, rows, x):
        ready[n & (SLOTS - 1), v, q, rows, :] = x

    triple_sums(
        makers, (FIRST_ORDER, None) * 2, shift, even, odd, three, last,
        enter, emit, lambda n: copy(n).start(),
    )
    for n in range(STEPS + 1 - SLOTS, STEPS + 1):
        copy(jnp.int32(n)).wait()
    for out in outs:
        out.wait()


SLOTS = 4
LINES = [
    [pltpu.VMEM((CHUNK, 88, NY), F32)] * 4,
    [pltpu.VMEM((CHUNK, 88, NY), F32)] * 4,
    [pltpu.VMEM((CHUNK, 64, NY), F32)] * 4,
    [pltpu.VMEM((2, OWN, NY), F32)] * 4,
]
SMALL = pl.BlockSpec(memory_space=pltpu.SMEM)
FAR = pl.BlockSpec(memory_space=pltpu.HBM)
NEAR = pl.BlockSpec(memory_space=pltpu.VMEM)
WINDOW = pltpu.VMEM((NZ, WIN, NY), BF16)
PLANES = pltpu.VMEM((4, PAGES, OWN, NY), F32)
RAW = pltpu.VMEM((3, NZ, WIN, NY), F32)


def in_vmem(x):
    return pltpu.with_memory_space_constraint(x, pltpu.VMEM)


def window_kernel(core, template, out, held, sem):
    rows = pl.ds(pl.multiple_of(core[0] * (NX - WIN), 8), WIN)
    fetch = pltpu.make_async_copy(template.at[:, rows], held, sem)
    fetch.start()
    fetch.wait()
    window = held[...]
    for d in range(32):
        out[d] = window


def window_copies(core, template):
    return pl.pallas_call(
        window_kernel,
        out_shape=pltpu.VMEM((32, 3, WIN, NY), BF16),
        in_specs=[SMALL, FAR],
        out_specs=NEAR,
        scratch_shapes=[pltpu.VMEM((3, WIN, NY), BF16), pltpu.SemaphoreType.DMA],
        compiler_params=pltpu.CompilerParams(vmem_limit_bytes=2 << 20),
        cost_estimate=pl.CostEstimate(flops=1, bytes_accessed=10**6, transcendentals=0),
        name="window_copies",
    )(core, in_hbm(template))


def moving_planes(idx, ja, jb):
    return pl.pallas_call(
        moving_kernel,
        out_shape=[pltpu.HBM((4, PAGES, OWN, NY), F32)] + [pltpu.HBM((8, 3, OWN, NY), F32)] * 4,
        in_specs=[SMALL, FAR, FAR],
        out_specs=[FAR] * 5,
        scratch_shapes=[
            WINDOW,
            WINDOW,
            pltpu.VMEM((NZ, WIN, NY), F32),
            *LINES,
            pltpu.VMEM((SLOTS, 4, 2 * CHUNK, OWN, NY), F32),
            pltpu.SemaphoreType.DMA((2, PARTS)),
            pltpu.SemaphoreType.DMA((32,)),
            pltpu.SemaphoreType.DMA((SLOTS,)),
        ],
        compiler_params=pltpu.CompilerParams(vmem_limit_bytes=24 << 20),
        cost_estimate=pl.CostEstimate(flops=4 * 10**9, bytes_accessed=6 * 10**6, transcendentals=0),
        name="moving_planes",
    )(idx, in_hbm(ja), in_hbm(jb))


def template_kernel(
    idx, i_hbm, ja_hbm, jb_hbm, plane, raw, iext_ref,
    i_ref, ja_ref, jb_ref, even, odd, three, last, in_sem, i_sem,
):
    shift = pl.multiple_of(idx[0] * 8, 8)
    fetches = window_fetches(idx[0], ((ja_hbm, ja_ref), (jb_hbm, jb_ref)), in_sem)
    for p in range(PARTS):
        part = pl.ds(p * PART, PART)
        fetches[p].append(pltpu.make_async_copy(i_hbm.at[part], i_ref.at[part], i_sem.at[p]))
        for fetch in fetches[p]:
            fetch.start()

    def makers(base):
        def wide(n, keep):
            f = load((i_ref, ja_ref, jb_ref)[n], base, CHUNK).astype(F32)
            if keep:
                raw[n, pl.ds(base, CHUNK)] = f.reshape(CHUNK, WIN, NY)
            return f

        def square():
            f = wide(0, True)
            return split(f * f)

        return [
            lambda: load(i_ref, base, CHUNK),
            square,
            lambda: split(wide(0, False) * wide(1, True)),
            lambda: split(wide(0, False) * wide(2, True)),
        ]

    def emit(v, n, q, rows, x):
        plane[v, 2 * CHUNK * n + q, rows, :] = x

    triple_sums(
        makers, (FIRST_ORDER, None, None, None), shift, even, odd, three, last,
        lambda n: wait_part(fetches, n), emit, lambda n: None,
    )
    start = idx[4] * 3 - 6
    for j in range(15):
        z = start + j
        inside = jnp.logical_and(z >= 0, z < NZ)
        page = raw[0, jnp.clip(z, 0, NZ - 1), pl.ds(shift, OWN), :]
        iext_ref[j] = jnp.where(inside, page, 0.0).astype(BF16)


def template_planes(idx, image, ja, jb):
    return pl.pallas_call(
        template_kernel,
        out_shape=[PLANES, RAW, jax.ShapeDtypeStruct((15, OWN, NY), BF16)],
        in_specs=[SMALL, FAR, FAR, FAR],
        out_specs=[NEAR] * 3,
        scratch_shapes=[
            WINDOW,
            WINDOW,
            WINDOW,
            *LINES,
            pltpu.SemaphoreType.DMA((2, PARTS)),
            pltpu.SemaphoreType.DMA((PARTS,)),
        ],
        compiler_params=pltpu.CompilerParams(vmem_limit_bytes=16 << 20),
        cost_estimate=pl.CostEstimate(flops=4 * 10**9, bytes_accessed=5 * 10**6, transcendentals=0),
        name="template_planes",
    )(idx, image, in_hbm(ja), in_hbm(jb))


def factor_kernel(kb, idx, iplane, jplane, raw, out, cc_ref):
    shift = pl.multiple_of(idx[0] * 8, 8)
    eps_b = EPSILON * COUNT
    eps_bc = EPSILON * COUNT**2

    def block(t, cc):
        slab = slab_of(idx, kb, t // 2, t % 2)
        first = slab * 3
        for r in range(OWN // 8):
            part = pl.ds(r * 8, 8)

            def boxes(ref, v):
                pages = [ref[v, first + 2 + p, part, :] for p in range(9)]
                return [pages[j] + pages[j + 3] + pages[j + 6] for j in range(3)]

            own = pl.ds(shift + r * 8, 8)
            si, sii = boxes(iplane, 0), boxes(iplane, 1)
            var_i = [sii[j] - si[j] * si[j] for j in range(3)]
            slope = [
                (raw[0, first + j, own, :] - si[j] * FIRST_ORDER) / (var_i[j] + eps_b)
                for j in range(3)
            ]
            total = [None] * 3
            for n in range(2):
                sj, sjj = boxes(jplane, 2 * n), boxes(jplane, 2 * n + 1)
                sij = boxes(iplane, 2 + n)
                for j in range(3):
                    var_j = sjj[j] - sj[j] * sj[j]
                    cross = sij[j] - si[j] * sj[j]
                    gain = cross / (var_i[j] * var_j + eps_bc)
                    cc = cc + cross * gain
                    moved = raw[1 + n, first + j, own, :] - sj[j] * FIRST_ORDER - cross * slope[j]
                    term = gain * moved
                    total[j] = term if n == 0 else total[j] + term
            for j in range(3):
                out[t, j, part, :] = total[j]
        return cc

    cc_ref[...] = lax.fori_loop(0, 8, block, jnp.zeros((8, NY), F32))


def factors(kb, idx, iplane, jplane, raw):
    return pl.pallas_call(
        functools.partial(factor_kernel, kb),
        out_shape=[
            jax.ShapeDtypeStruct((8, 3, OWN, NY), F32),
            jax.ShapeDtypeStruct((8, NY), F32),
        ],
        in_specs=[SMALL, NEAR, NEAR, NEAR],
        out_specs=[NEAR] * 2,
        compiler_params=pltpu.CompilerParams(vmem_limit_bytes=4 << 20),
        cost_estimate=pl.CostEstimate(flops=4 * 10**8, bytes_accessed=10**6, transcendentals=0),
        name="factors",
    )(idx, in_vmem(iplane), in_vmem(jplane), in_vmem(raw))


CC_ROWS = 8
SIDE = 6 * OWN
CENTRE = 6 * OWN + CC_ROWS


def twice_slopes(here):
    row = lax.broadcasted_iota(jnp.int32, (NX, NY), 0)
    lane = lax.broadcasted_iota(jnp.int32, (NX, NY), 1)
    below = jnp.where(row == NX - 1, 0.0, pltpu.roll(here, NX - 1, 0))
    above = jnp.where(row == 0, 0.0, pltpu.roll(here, 1, 0))
    right = jnp.where(lane == NY - 1, 0.0, pltpu.roll(here, NY - 1, 1))
    left = jnp.where(lane == 0, 0.0, pltpu.roll(here, 1, 1))
    return below - above, right - left


def slope_kernel(idx, iown_ref, iother_ref, slope_ref, image):
    mine = pl.multiple_of(idx[0] * OWN, 8)
    others = pl.multiple_of((1 - idx[0]) * OWN, 8)
    for p in range(15):
        image[p, pl.ds(mine, OWN), :] = iown_ref[p].astype(F32)
        image[p, pl.ds(others, OWN), :] = iother_ref[p].astype(F32)
    scale = COUNT
    for p in range(13):
        sx, sy = twice_slopes(image[p + 1])
        slope_ref[0, p] = (image[p + 2] - image[p]) * scale
        slope_ref[1, p] = sx * scale
        slope_ref[2, p] = sy * scale


def slopes(idx, iown, iother):
    return pl.pallas_call(
        slope_kernel,
        out_shape=pltpu.VMEM((3, 13, NX, NY), F32),
        in_specs=[SMALL, NEAR, NEAR],
        out_specs=NEAR,
        scratch_shapes=[pltpu.VMEM((15, NX, NY), F32)],
        compiler_params=pltpu.CompilerParams(vmem_limit_bytes=6 << 20),
        cost_estimate=pl.CostEstimate(flops=10**6, bytes_accessed=10**6, transcendentals=0),
        name="slopes",
    )(idx, iown, iother)


def smooth_kernel(
    idx, own_ref, twin_ref, other_ref, slope_ref, u_ref, adv_ref, m_ref, st_ref, ext, mext, prod,
):
    core, sub, xh = idx[0], idx[4], idx[5]
    mine = pl.multiple_of(core * OWN, 8)
    others = pl.multiple_of((1 - core) * OWN, 8)

    def centre(rows, ref):
        for j in range(3):
            ext[5 + j, rows, :] = ref[pl.ds(j * OWN, OWN), :]
            mext[1 + j, rows, :] = ref[pl.ds((3 + j) * OWN, OWN), :]

    def sides(rows, low, high):
        for d, (ref, at) in enumerate((low, high)):
            for j in range(5):
                z = sub * 3 + (j - 5 if d == 0 else j + 3)
                inside = jnp.logical_and(z >= 0, z < NZ)
                page = ref[pl.ds(at + j * OWN, OWN), :]
                ext[j if d == 0 else 8 + j, rows, :] = jnp.where(inside, page, 0.0)
            z = sub * 3 + (-1 if d == 0 else 3)
            inside = jnp.logical_and(z >= 0, z < NZ)
            page = ref[pl.ds(at + 5 * OWN, OWN), :]
            mext[0 if d == 0 else 4, rows, :] = jnp.where(inside, page, 0.0)

    my_rows, other_rows = pl.ds(mine, OWN), pl.ds(others, OWN)
    centre(my_rows, own_ref)
    centre(other_rows, other_ref)

    @pl.when(xh == 0)
    def _():
        sides(my_rows, (own_ref, CENTRE), (twin_ref, 0))
        sides(other_rows, (other_ref, CENTRE), (other_ref, CENTRE + SIDE))

    @pl.when(xh == 1)
    def _():
        sides(my_rows, (twin_ref, 0), (own_ref, CENTRE))
        sides(other_rows, (other_ref, CENTRE + SIDE), (other_ref, CENTRE))

    weights = [math.exp(-o * o / (2.0 * VARIANCE)) for o in range(-REACH, REACH + 1)]
    norm = sum(weights)
    weights = [w / norm for w in weights]

    def matrix(n):
        r = lax.broadcasted_iota(jnp.int32, (n, n), 0)
        c = lax.broadcasted_iota(jnp.int32, (n, n), 1)
        d = (r - c).astype(F32)
        return jnp.where(jnp.abs(r - c) <= REACH, jnp.exp(-d * d / (2.0 * VARIANCE)) / norm, 0.0)

    def halves(x):
        high = x.astype(BF16)
        return high, (x - high.astype(F32)).astype(BF16)

    high, low = halves(matrix(NX))
    gx3 = jnp.concatenate([high, high, low], axis=1)
    high, low = halves(matrix(NY))
    gy3 = jnp.concatenate([high, high, low], axis=0)
    for p in range(13):
        for d in range(3):
            prod[d, p] = ext[p] * slope_ref[d, p]
    square = jnp.zeros((NX, NY), F32)
    image_square = jnp.zeros((NX, NY), F32)
    mean = 1.0 / DEVICES
    for j in range(3):
        m = mext[1 + j] * mean
        sx, sy = twice_slopes(m)
        slopes = ((mext[2 + j] - mext[j]) * mean, sx, sy)
        image_square = image_square + m * m
        moved = None
        for d in range(3):
            acc = prod[d, j] * weights[0]
            for o in range(1, 11):
                acc = acc + prod[d, j + o] * weights[o]
            acc = dot(jnp.concatenate([*halves(acc), halves(acc)[0]], axis=1), gy3)
            high, low = halves(acc)
            acc = dot(gx3, jnp.concatenate([high, low, high], axis=0))
            u = acc * mean
            u_ref[j, d] = u
            square = square + u * u
            term = u * slopes[d]
            moved = term if d == 0 else moved + term
        adv_ref[j] = moved * 0.5
        m_ref[j] = m
    tail = pl.ds(6 * OWN, CC_ROWS)
    cc = jnp.sum(own_ref[tail, :] + other_ref[tail, :])
    one = lax.broadcasted_iota(jnp.int32, (1, NY), 1)
    st_ref[...] = jnp.where(
        one == 0, jnp.sum(square), jnp.where(one == 1, jnp.sum(image_square), cc)
    )


def smooth_slab(idx, own, twin, other, slope):
    vm = pl.BlockSpec(memory_space=pltpu.VMEM)
    return pl.pallas_call(
        smooth_kernel,
        out_shape=[
            jax.ShapeDtypeStruct((3, 3, NX, NY), F32),
            jax.ShapeDtypeStruct((3, NX, NY), F32),
            jax.ShapeDtypeStruct((3, NX, NY), F32),
            jax.ShapeDtypeStruct((1, NY), F32),
        ],
        in_specs=[pl.BlockSpec(memory_space=pltpu.SMEM), vm, vm, vm, vm],
        out_specs=[vm] * 4,
        scratch_shapes=[
            pltpu.VMEM((13, NX, NY), F32),
            pltpu.VMEM((5, NX, NY), F32),
            pltpu.VMEM((3, 13, NX, NY), F32),
        ],
        compiler_params=pltpu.CompilerParams(vmem_limit_bytes=24 << 20),
        cost_estimate=pl.CostEstimate(flops=10**8, bytes_accessed=3 * 10**6, transcendentals=0),
        name="smooth_slab",
    )(idx, own, twin, other, slope)


def finish_kernel(rows_ref, u_ref, adv_ref, m_ref, v_ref, t_ref, sim_ref):
    totals = jnp.sum(rows_ref[...], axis=0, keepdims=True)
    cells = NZ * NX * NY
    velocity_scale = STEP_LENGTH / jnp.sqrt(totals[:, 0:1] / cells + EPSILON)
    image_scale = 1.0 / jnp.sqrt(totals[:, 1:2] / cells + EPSILON)
    sim_ref[...] = totals[:, 2:3] * (0.5 / (DEVICES * cells))
    for j in range(3):
        for d in range(3):
            v_ref[j, d] = u_ref[j, d] * velocity_scale
        t_ref[j] = (m_ref[j] - adv_ref[j] * velocity_scale) * image_scale


def finish(rows, u, advected, m):
    vm = pl.BlockSpec(memory_space=pltpu.VMEM)
    return pl.pallas_call(
        finish_kernel,
        out_shape=[
            jax.ShapeDtypeStruct((3, 3, NX, NY), F32),
            jax.ShapeDtypeStruct((3, NX, NY), F32),
            jax.ShapeDtypeStruct((1, 1), F32),
        ],
        in_specs=[vm] * 4,
        out_specs=[vm] * 3,
        compiler_params=pltpu.CompilerParams(vmem_limit_bytes=12 << 20),
        name="finish",
    )(rows, u, advected, m)


def after(value, *others):
    return lax.optimization_barrier((value, *others))[0]


def round_one(blocks):
    return [permute(blocks[k], first_round(k)) for k in (1, 2, 3)]


def round_two(total):
    parts = [total[2 * k : 2 * k + 2] for k in range(4)]
    got = []
    for k in (2, 1, 3):
        got.append(permute(parts[k], second_round(k)))
    return parts[0] + got[0] + got[1] + got[2]


def step(template, subjects):
    grp = lax.axis_index("grp")
    sub = lax.axis_index("sub")
    core = grp % 2
    xl, y, z = sub // 16, (sub // 4) % 4, sub % 4
    first = jnp.where(core == 0, z, y)
    second = jnp.where(core == 0, y, z)
    idx = jnp.stack([core, first, second, xl, sub, grp // 2]).astype(jnp.int32)

    keep = subjects[0]
    take = permute(keep, CORE_PAIRS)
    copies = window_copies(core.astype(jnp.int32).reshape(1), template)
    image = lax.all_to_all(copies, "sub", 0, 0, tiled=True).reshape(NZ, WIN, NY)

    jplane, *j_blocks = moving_planes(idx, keep, take)
    j_got = round_one(j_blocks)
    iplane, raw, i_half = template_planes(idx, image, keep, take)
    f_blocks, f_got, cc = [None] * 4, [None] * 4, None
    for k in (2, 1, 3, 0):
        f_blocks[k], part = factors(k, idx, iplane, jplane, raw)
        cc = part if cc is None else cc + part
        if k:
            f_got[k] = permute(f_blocks[k], first_round(k))
    j_own = after(j_blocks[0], cc)
    j_total = j_own + j_got[0] + j_got[1] + j_got[2]
    i_other = permute(i_half, CORE_PAIRS)
    slope = slopes(idx, i_half, i_other)
    f_total = f_blocks[0] + f_got[1] + f_got[2] + f_got[3]
    part = round_two(jnp.concatenate([f_total, j_total], axis=1))
    both = jnp.concatenate(
        [part.reshape(2, 6 * OWN, NY), jnp.broadcast_to(cc[None], (2, CC_ROWS, NY))], axis=1
    )
    half = both[0]
    for k in (2, 1, 3):
        half = half + permute(both[k % 2], third_round(k))

    f_half = half[: 3 * OWN]
    m_half = half[3 * OWN : 6 * OWN]
    low = grp < 2
    near = jnp.concatenate(
        [f_half, jnp.where(low, m_half[2 * OWN :], m_half[:OWN])], axis=0
    )
    far = jnp.where(low, f_half[OWN:], f_half[: 2 * OWN])
    near = permute(near, slab_shift(1))
    far = permute(far, slab_shift(2))
    near_f, near_m = near[: 3 * OWN], near[3 * OWN :]
    f_side = jnp.where(
        low, jnp.concatenate([far, near_f], axis=0), jnp.concatenate([near_f, far], axis=0)
    )
    side = jnp.concatenate([f_side, near_m], axis=0)
    twin = permute(side, TWIN_PAIRS)
    own = jnp.concatenate([half, side], axis=0)
    other = permute(jnp.concatenate([own, twin], axis=0), CORE_PAIRS)
    u, advected, m, stats = smooth_slab(idx, own, twin, other, slope)
    rows = lax.all_to_all(jnp.broadcast_to(stats[None], (32, 1, NY)), "sub", 0, 0, tiled=True)
    velocity, new_template, similarity = finish(rows.reshape(32, NY), u, advected, m)
    return velocity, new_template, similarity.reshape(())


def solution(mesh):
    return jax.shard_map(
        step,
        mesh=mesh,
        in_specs=(P("sub", None, None), P(("grp", "sub"), None, None, None)),
        out_specs=(P("sub", None, None, None), P("sub", None, None), P()),
        check_vma=False,
    )
```

profile of v0, /device:TPU:0, one launch (start us, length us, event | category | flops | bytes accessed | tf_op | source)
XLA Modules:
  0.0 133.0 jit_solution(3101238743714517707)
XLA Ops:
  0.6 0.1 collective-permute-start
  0.7 2.1 %window_copies.1 = bf16[32,3,56,128]{3,2,1,0:T(8,128)(2,1)} custom-call(s32[1]{0:T(128)} %bitcast.core, bf16[3,96,128]{2,1,0:T(8,128)(2,1)} %template.1), custom_call_target="tpu_custom_call" | custom-call | flops 1 | bytes 1000000 | tf_op jit(solution)/shard_map/window_copies/pallas_call | solution.py:313
  2.8 9.4 %all-to-all-start = ((bf16[32,3,56,128]{3,2,1,0:T(8,128)(2,1)}), bf16[32,3,56,128]{3,2,1,0:T(8,128)(2,1)S(1)}, u32[]{:S(2)}, u32[]{:S(2)}) async-start(bf16[32,3,56,128]{3,2,1,0:T(8,128)(2,1)} %window_copies.1), calls=%async_computation | async-start | bytes 2752512 | tf_op jit(solution)/shard_map/all_to_all | solution.py:679
  12.3 0.1 stack.27.idx
  12.4 0.0 collective-permute-done.jb_hbm
  12.4 9.7 %moving_planes.1 = (f32[4,104,48,128]{3,2,1,0:T(8,128)}, f32[8,3,48,128]{3,2,1,0:T(8,128)}, f32[8,3,48,128]{3,2,1,0:T(8,128)}, f32[8,3,48,128]{3,2,1,0:T(8,128)}, f32[8,3,48,128]{3,2,1,0:T(8,128)}) custom-call(s32[6]{0:T(128)S(1)} %stack.27.idx, bf16[96,96,128]{2,1,0:T(8,128)(2,1)} %bitcast.24, bf16[96,96,128]{2,1,0:T(8,128)(2,1)} %collective-permute-done.jb_hbm), custom_call_target="tpu_custom_call" | custom-call | flops 4000000000 | bytes 6000000 | tf_op jit(solution)/shard_map/moving_planes/pallas_call | solution.py:326
  22.0 1.9 %collective-permute-start.4 = (f32[8,3,48,128]{3,2,1,0:T(8,128)}, f32[8,3,48,128]{3,2,1,0:T(8,128)S(1)}, u32[]{:S(2)}, u32[]{:S(2)}) collective-permute-start(f32[8,3,48,128]{3,2,1,0:T(8,128)} %get-tuple-element.40), channel_id=1, source_target_pairs={{0,1},{1,2},{2,3},{3,0},{4,5},{5,6},{6,7},{7,4},{8,9},{9,10},{10,1... | collective-permute-start | bytes 1769480 | tf_op jit(solution)/shard_map/ppermute | solution.py:76
  23.9 2.7 %collective-permute-start.5 = (f32[8,3,48,128]{3,2,1,0:T(8,128)}, f32[8,3,48,128]{3,2,1,0:T(8,128)S(1)}, u32[]{:S(2)}, u32[]{:S(2)}) collective-permute-start(f32[8,3,48,128]{3,2,1,0:T(8,128)} %get-tuple-element.41), channel_id=1, source_target_pairs={{0,2},{1,3},{2,0},{3,1},{4,6},{5,7},{6,4},{7,5},{8,10},{9,11},{10,... | collective-permute-start | bytes 1769480 | tf_op jit(solution)/shard_map/ppermute | solution.py:76
  26.6 1.5 %collective-permute-start.6 = (f32[8,3,48,128]{3,2,1,0:T(8,128)}, f32[8,3,48,128]{3,2,1,0:T(8,128)S(1)}, u32[]{:S(2)}, u32[]{:S(2)}) collective-permute-start(f32[8,3,48,128]{3,2,1,0:T(8,128)} %get-tuple-element.42), channel_id=1, source_target_pairs={{0,3},{1,0},{2,1},{3,2},{4,7},{5,4},{6,5},{7,6},{8,11},{9,8},{10,9... | collective-permute-start | bytes 1769480 | tf_op jit(solution)/shard_map/ppermute | solution.py:76
  28.0 5.1 %all-to-all-done = bf16[32,3,56,128]{3,2,1,0:T(8,128)(2,1)S(1)} async-done(((bf16[32,3,56,128]{3,2,1,0:T(8,128)(2,1)}), bf16[32,3,56,128]{3,2,1,0:T(8,128)(2,1)S(1)}, u32[]{:S(2)}, u32[]{:S(2)}) %all-to-all-start) | async-done | bytes 1376288 | tf_op jit(solution)/shard_map/all_to_all | solution.py:679
  33.1 0.0 copy-start
  33.1 8.1 %template_planes.1 = (f32[4,104,48,128]{3,2,1,0:T(8,128)S(1)}, f32[3,96,56,128]{3,2,1,0:T(8,128)S(1)}, bf16[15,48,128]{2,1,0:T(8,128)(2,1)S(1)}) custom-call(s32[6]{0:T(128)S(1)} %stack.27.idx, bf16[96,56,128]{2,1,0:T(8,128)(2,1)S(1)} %bitcast.18, bf16[96,96,128]{2,1,0:T(8,128)(2,1)} %bitcast.25, bf16[96,96,128]{2,1,0:T(8,128)(2,1)} %collective-permute-done.jb_hbm), custom_call_target="tpu_custom_call" | custom-call | flops 4000000000 | bytes 5000000 | tf_op jit(solution)/shard_map/template_planes/pallas_call | solution.py:393
  41.3 0.0 copy-done
  41.3 1.9 %factors.5 = (f32[8,3,48,128]{3,2,1,0:T(8,128)S(1)}, f32[8,128]{1,0:T(8,128)S(1)}) custom-call(s32[6]{0:T(128)S(1)} %stack.27.idx, f32[4,104,48,128]{3,2,1,0:T(8,128)S(1)} %get-tuple-element.27.iplane, f32[4,104,48,128]{3,2,1,0:T(8,128)S(1)} %copy-done, f32[3,96,56,128]{3,2,1,0:T(8,128)S(1)} %get-tuple-element.29.raw), custom_call_target="tpu_custom_call" | custom-call | flops 400000000 | bytes 1000000 | tf_op jit(solution)/shard_map/factors/pallas_call | solution.py:454
  43.1 1.1 collective-permute-start.1
  44.3 1.8 %factors.6 = (f32[8,3,48,128]{3,2,1,0:T(8,128)S(1)}, f32[8,128]{1,0:T(8,128)S(1)}) custom-call(s32[6]{0:T(128)S(1)} %stack.27.idx, f32[4,104,48,128]{3,2,1,0:T(8,128)S(1)} %get-tuple-element.27.iplane, f32[4,104,48,128]{3,2,1,0:T(8,128)S(1)} %copy-done, f32[3,96,56,128]{3,2,1,0:T(8,128)S(1)} %get-tuple-element.29.raw), custom_call_target="tpu_custom_call" | custom-call | flops 400000000 | bytes 1000000 | tf_op jit(solution)/shard_map/factors/pallas_call | solution.py:454
  46.1 1.8 %collective-permute-start.2 = (f32[8,3,48,128]{3,2,1,0:T(8,128)S(1)}, f32[8,3,48,128]{3,2,1,0:T(8,128)S(1)}, u32[]{:S(2)}, u32[]{:S(2)}) collective-permute-start(f32[8,3,48,128]{3,2,1,0:T(8,128)S(1)} %get-tuple-element.32), channel_id=1, source_target_pairs={{0,2},{1,3},{2,0},{3,1},{4,6},{5,7},{6,4},{7,5},{8,10},{9,11},{10,... | collective-permute-start | bytes 1769480 | tf_op jit(solution)/shard_map/ppermute | solution.py:76
  47.9 1.8 %factors.7 = (f32[8,3,48,128]{3,2,1,0:T(8,128)S(1)}, f32[8,128]{1,0:T(8,128)S(1)}) custom-call(s32[6]{0:T(128)S(1)} %stack.27.idx, f32[4,104,48,128]{3,2,1,0:T(8,128)S(1)} %get-tuple-element.27.iplane, f32[4,104,48,128]{3,2,1,0:T(8,128)S(1)} %copy-done, f32[3,96,56,128]{3,2,1,0:T(8,128)S(1)} %get-tuple-element.29.raw), custom_call_target="tpu_custom_call" | custom-call | flops 400000000 | bytes 1000000 | tf_op jit(solution)/shard_map/factors/pallas_call | solution.py:454
  49.7 0.0 collective-permute-done.4
  49.7 0.0 copy-start.1
  49.7 2.0 %collective-permute-start.3 = (f32[8,3,48,128]{3,2,1,0:T(8,128)S(1)}, f32[8,3,48,128]{3,2,1,0:T(8,128)S(1)}, u32[]{:S(2)}, u32[]{:S(2)}) collective-permute-start(f32[8,3,48,128]{3,2,1,0:T(8,128)S(1)} %get-tuple-element.33), channel_id=1, source_target_pairs={{0,3},{1,0},{2,1},{3,2},{4,7},{5,4},{6,5},{7,6},{8,11},{9,8},{10,9... | collective-permute-start | bytes 1769480 | tf_op jit(solution)/shard_map/ppermute | solution.py:76
  51.7 1.8 %factors.4 = (f32[8,3,48,128]{3,2,1,0:T(8,128)S(1)}, f32[8,128]{1,0:T(8,128)S(1)}) custom-call(s32[6]{0:T(128)S(1)} %stack.27.idx, f32[4,104,48,128]{3,2,1,0:T(8,128)S(1)} %get-tuple-element.27.iplane, f32[4,104,48,128]{3,2,1,0:T(8,128)S(1)} %copy-done, f32[3,96,56,128]{3,2,1,0:T(8,128)S(1)} %get-tuple-element.29.raw), custom_call_target="tpu_custom_call" | custom-call | flops 400000000 | bytes 1000000 | tf_op jit(solution)/shard_map/factors/pallas_call | solution.py:454
  53.5 0.0 collective-permute-done.5
  53.5 0.0 collective-permute-done.6
  53.5 0.0 copy-done.1
  53.5 0.2 add_add_fusion
  53.7 6.9 %collective-permute-done.1 = f32[8,3,48,128]{3,2,1,0:T(8,128)S(1)} collective-permute-done((f32[8,3,48,128]{3,2,1,0:T(8,128)S(1)}, f32[8,3,48,128]{3,2,1,0:T(8,128)S(1)}, u32[]{:S(2)}, u32[]{:S(2)}) %collective-permute-start.1) | collective-permute-done | bytes 589856 | tf_op jit(solution)/shard_map/ppermute | solution.py:76
  60.6 0.0 collective-permute-done.2
  60.6 2.8 %collective-permute-done.3 = f32[8,3,48,128]{3,2,1,0:T(8,128)S(1)} collective-permute-done((f32[8,3,48,128]{3,2,1,0:T(8,128)S(1)}, f32[8,3,48,128]{3,2,1,0:T(8,128)S(1)}, u32[]{:S(2)}, u32[]{:S(2)}) %collective-permute-start.3) | collective-permute-done | bytes 589856 | tf_op jit(solution)/shard_map/ppermute | solution.py:76
  63.4 0.1 add_add_fusion.1
  63.6 0.1 fusion.5
  63.7 2.4 %collective-permute-start.7 = (f32[2,6,48,128]{3,2,1,0:T(8,128)S(1)}, f32[2,6,48,128]{3,2,1,0:T(8,128)S(1)}, u32[]{:S(2)}, u32[]{:S(2)}) collective-permute-start(f32[2,6,48,128]{3,2,1,0:T(8,128)S(1)} %get-tuple-element.51), channel_id=1, source_target_pairs={{0,8},{1,9},{2,10},{3,11},{4,12},{5,13},{6,14},{7,15},{8,0},{9,1},... | collective-permute-start | bytes 884744 | tf_op jit(solution)/shard_map/ppermute | solution.py:76
  66.1 0.4 collective-permute-start.8
  66.5 2.8 %collective-permute-start.9 = (f32[2,6,48,128]{3,2,1,0:T(8,128)S(1)}, f32[2,6,48,128]{3,2,1,0:T(8,128)S(1)}, u32[]{:S(2)}, u32[]{:S(2)}) collective-permute-start(f32[2,6,48,128]{3,2,1,0:T(8,128)S(1)} %get-tuple-element.52), channel_id=1, source_target_pairs={{0,12},{1,13},{2,14},{3,15},{4,0},{5,1},{6,2},{7,3},{8,4},{9,5},{1... | collective-permute-start | bytes 884744 | tf_op jit(solution)/shard_map/ppermute | solution.py:76
  69.3 2.8 %collective-permute-done.7 = f32[2,6,48,128]{3,2,1,0:T(8,128)S(1)} collective-permute-done((f32[2,6,48,128]{3,2,1,0:T(8,128)S(1)}, f32[2,6,48,128]{3,2,1,0:T(8,128)S(1)}, u32[]{:S(2)}, u32[]{:S(2)}) %collective-permute-start.7) | collective-permute-done | bytes 294944 | tf_op jit(solution)/shard_map/ppermute | solution.py:76
  72.1 3.1 %collective-permute-done.8 = f32[2,6,48,128]{3,2,1,0:T(8,128)S(1)} collective-permute-done((f32[2,6,48,128]{3,2,1,0:T(8,128)S(1)}, f32[2,6,48,128]{3,2,1,0:T(8,128)S(1)}, u32[]{:S(2)}, u32[]{:S(2)}) %collective-permute-start.8) | collective-permute-done | bytes 294944 | tf_op jit(solution)/shard_map/ppermute | solution.py:76
  75.1 0.0 collective-permute-done.9
  75.1 0.1 fusion.4
  75.2 2.8 %collective-permute-start.10 = (f32[296,128]{1,0:T(8,128)S(1)}, f32[296,128]{1,0:T(8,128)S(1)}, u32[]{:S(2)}, u32[]{:S(2)}) collective-permute-start(f32[296,128]{1,0:T(8,128)S(1)} %get-tuple-element.54), channel_id=1, source_target_pairs={{0,64},{1,65},{2,66},{3,67},{4,68},{5,69},{6,70},{7,71},{8,72},{9,... | collective-permute-start | bytes 454664 | tf_op jit(solution)/shard_map/ppermute | solution.py:76
  78.0 10.1 %collective-permute-start.11 = (f32[296,128]{1,0:T(8,128)S(1)}, f32[296,128]{1,0:T(8,128)S(1)}, u32[]{:S(2)}, u32[]{:S(2)}) collective-permute-start(f32[296,128]{1,0:T(8,128)S(1)} %get-tuple-element.55), channel_id=1, source_target_pairs={{0,16},{1,17},{2,18},{3,19},{4,20},{5,21},{6,22},{7,23},{8,24},{9,... | collective-permute-start | bytes 454664 | tf_op jit(solution)/shard_map/ppermute | solution.py:76
  88.2 0.6 collective-permute-start.12
  88.7 0.0 collective-permute-done.10
  88.7 3.2 %collective-permute-done.11 = f32[296,128]{1,0:T(8,128)S(1)} collective-permute-done((f32[296,128]{1,0:T(8,128)S(1)}, f32[296,128]{1,0:T(8,128)S(1)}, u32[]{:S(2)}, u32[]{:S(2)}) %collective-permute-start.11) | collective-permute-done | bytes 151584 | tf_op jit(solution)/shard_map/ppermute | solution.py:76
  91.9 2.6 %collective-permute-done.12 = f32[296,128]{1,0:T(8,128)S(1)} collective-permute-done((f32[296,128]{1,0:T(8,128)S(1)}, f32[296,128]{1,0:T(8,128)S(1)}, u32[]{:S(2)}, u32[]{:S(2)}) %collective-permute-start.12) | collective-permute-done | bytes 151584 | tf_op jit(solution)/shard_map/ppermute | solution.py:76
  94.5 0.1 add_add_fusion.2
  94.6 0.4 collective-permute-start.14
  95.1 4.8 %collective-permute-start.13 = (f32[96,128]{1,0:T(8,128)S(1)}, f32[96,128]{1,0:T(8,128)S(1)}, u32[]{:S(2)}, u32[]{:S(2)}) collective-permute-start(f32[96,128]{1,0:T(8,128)S(1)} %slice_select_fusion), channel_id=1, source_target_pairs={{0,2},{1,3},{2,4},{3,5},{4,6},{5,7},{6,8},{7,9},{8,10},{9,11},{10,... | collective-permute-start | bytes 147464 | tf_op jit(solution)/shard_map/ppermute | solution.py:76
  99.9 3.7 %collective-permute-done.14 = f32[192,128]{1,0:T(8,128)S(1)} collective-permute-done((f32[192,128]{1,0:T(8,128)S(1)}, f32[192,128]{1,0:T(8,128)S(1)}, u32[]{:S(2)}, u32[]{:S(2)}) %collective-permute-start.14) | collective-permute-done | bytes 98336 | tf_op jit(solution)/shard_map/ppermute | solution.py:76
  103.6 0.9 collective-permute-done.13
  104.5 5.3 %collective-permute-start.15 = (f32[288,128]{1,0:T(8,128)S(1)}, f32[288,128]{1,0:T(8,128)S(1)}, u32[]{:S(2)}, u32[]{:S(2)}) collective-permute-start(f32[288,128]{1,0:T(8,128)S(1)} %pad_maximum_fusion.4), channel_id=1, source_target_pairs={{0,64},{1,65},{2,66},{3,67},{4,68},{5,69},{6,70},{7,71},{8,72},{9,... | collective-permute-start | bytes 442376 | tf_op jit(solution)/shard_map/ppermute | solution.py:76
  109.9 3.1 %collective-permute-done.15.twin_ref = f32[288,128]{1,0:T(8,128)S(1)} collective-permute-done((f32[288,128]{1,0:T(8,128)S(1)}, f32[288,128]{1,0:T(8,128)S(1)}, u32[]{:S(2)}, u32[]{:S(2)}) %collective-permute-start.15) | collective-permute-done | bytes 147488 | tf_op jit(solution)/shard_map/ppermute | solution.py:76
  113.0 0.1 collective-permute-start.16
  113.1 0.5 collective-permute-start.17
  113.6 1.6 %collective-permute-done.17.iother_ref = bf16[15,48,128]{2,1,0:T(8,128)(2,1)S(1)} collective-permute-done((bf16[15,48,128]{2,1,0:T(8,128)(2,1)S(1)}, bf16[15,48,128]{2,1,0:T(8,128)(2,1)S(1)}, u32[]{:S(2)}, u32[]{:S(2)}) %collective-permute-start.17) | collective-permute-done | bytes 184352 | tf_op jit(solution)/shard_map/ppermute | solution.py:76
  115.2 1.0 slopes.1.slope_ref
  116.2 0.0 collective-permute-done.16.other_ref
  116.2 2.6 %smooth_slab.1 = (f32[3,3,96,128]{3,2,1,0:T(8,128)S(1)}, f32[3,96,128]{2,1,0:T(8,128)S(1)}, f32[3,96,128]{2,1,0:T(8,128)S(1)}, f32[1,128]{1,0:T(1,128)S(1)}) custom-call(s32[6]{0:T(128)S(1)} %stack.27.idx, f32[584,128]{1,0:T(8,128)S(1)} %pad_maximum_fusion.1.own_ref, f32[288,128]{1,0:T(8,128)S(1)} %collective-permute-done.15.twin_ref, ...), custom_call_target="tpu_custom_call" | custom-call | flops 100000000 | bytes 3000000 | tf_op jit(solution)/shard_map/smooth_slab/pallas_call | solution.py:602
  118.8 13.2 %all_to_all.10 = f32[32,1,128]{2,1,0:T(1,128)S(1)} all-to-all(f32[32,1,128]{2,1,0:T(1,128)S(1)} %broadcast_in_dim.16), channel_id=1, replica_groups=mesh['grp'=4,'sub'=32] {'sub'}, dimensions={0} | all-to-all | bytes 32768 | tf_op jit(solution)/shard_map/all_to_all | solution.py:721
  132.1 0.9 finish.1
  (14 shorter events, 0.2 us)
Async XLA Ops:
  0.6 11.7 %collective-permute-start = (bf16[96,96,128]{2,1,0:T(8,128)(2,1)}, bf16[96,96,128]{2,1,0:T(8,128)(2,1)}, u32[]{:S(2)}, u32[]{:S(2)}) collective-permute-start(bf16[96,96,128]{2,1,0:T(8,128)(2,1)} %bitcast.23), channel_id=1, source_target_pairs={{0,32},{1,33},{2,34},{3,35},{4,36},{5,37},{6,38},{7,39},{8,40},{9,... | collective-permute-start | bytes 7077896 | tf_op jit(solution)/shard_map/ppermute | solution.py:76
  2.8 30.3 %all-to-all-start = ((bf16[32,3,56,128]{3,2,1,0:T(8,128)(2,1)}), bf16[32,3,56,128]{3,2,1,0:T(8,128)(2,1)S(1)}, u32[]{:S(2)}, u32[]{:S(2)}) async-start(bf16[32,3,56,128]{3,2,1,0:T(8,128)(2,1)} %window_copies.1), calls=%async_computation | async-start | bytes 2752512 | tf_op jit(solution)/shard_map/all_to_all | solution.py:679
  22.0 27.7 %collective-permute-start.4 = (f32[8,3,48,128]{3,2,1,0:T(8,128)}, f32[8,3,48,128]{3,2,1,0:T(8,128)S(1)}, u32[]{:S(2)}, u32[]{:S(2)}) collective-permute-start(f32[8,3,48,128]{3,2,1,0:T(8,128)} %get-tuple-element.40), channel_id=1, source_target_pairs={{0,1},{1,2},{2,3},{3,0},{4,5},{5,6},{6,7},{7,4},{8,9},{9,10},{10,1... | collective-permute-start | bytes 1769480 | tf_op jit(solution)/shard_map/ppermute | solution.py:76
  23.9 29.6 %collective-permute-start.5 = (f32[8,3,48,128]{3,2,1,0:T(8,128)}, f32[8,3,48,128]{3,2,1,0:T(8,128)S(1)}, u32[]{:S(2)}, u32[]{:S(2)}) collective-permute-start(f32[8,3,48,128]{3,2,1,0:T(8,128)} %get-tuple-element.41), channel_id=1, source_target_pairs={{0,2},{1,3},{2,0},{3,1},{4,6},{5,7},{6,4},{7,5},{8,10},{9,11},{10,... | collective-permute-start | bytes 1769480 | tf_op jit(solution)/shard_map/ppermute | solution.py:76
  26.6 27.0 %collective-permute-start.6 = (f32[8,3,48,128]{3,2,1,0:T(8,128)}, f32[8,3,48,128]{3,2,1,0:T(8,128)S(1)}, u32[]{:S(2)}, u32[]{:S(2)}) collective-permute-start(f32[8,3,48,128]{3,2,1,0:T(8,128)} %get-tuple-element.42), channel_id=1, source_target_pairs={{0,3},{1,0},{2,1},{3,2},{4,7},{5,4},{6,5},{7,6},{8,11},{9,8},{10,9... | collective-permute-start | bytes 1769480 | tf_op jit(solution)/shard_map/ppermute | solution.py:76
  33.1 8.1 %copy-start = (f32[4,104,48,128]{3,2,1,0:T(8,128)S(1)}, f32[4,104,48,128]{3,2,1,0:T(8,128)}, u32[]{:S(2)}) copy-start(f32[4,104,48,128]{3,2,1,0:T(8,128)} %get-tuple-element.28.jplane) | copy-start | bytes 30670852
  43.1 17.5 %collective-permute-start.1 = (f32[8,3,48,128]{3,2,1,0:T(8,128)S(1)}, f32[8,3,48,128]{3,2,1,0:T(8,128)S(1)}, u32[]{:S(2)}, u32[]{:S(2)}) collective-permute-start(f32[8,3,48,128]{3,2,1,0:T(8,128)S(1)} %get-tuple-element.31), channel_id=1, source_target_pairs={{0,1},{1,2},{2,3},{3,0},{4,5},{5,6},{6,7},{7,4},{8,9},{9,10},{10,1... | collective-permute-start | bytes 1769480 | tf_op jit(solution)/shard_map/ppermute | solution.py:76
  46.1 14.5 %collective-permute-start.2 = (f32[8,3,48,128]{3,2,1,0:T(8,128)S(1)}, f32[8,3,48,128]{3,2,1,0:T(8,128)S(1)}, u32[]{:S(2)}, u32[]{:S(2)}) collective-permute-start(f32[8,3,48,128]{3,2,1,0:T(8,128)S(1)} %get-tuple-element.32), channel_id=1, source_target_pairs={{0,2},{1,3},{2,0},{3,1},{4,6},{5,7},{6,4},{7,5},{8,10},{9,11},{10,... | collective-permute-start | bytes 1769480 | tf_op jit(solution)/shard_map/ppermute | solution.py:76
  49.7 3.8 %copy-start.1 = (f32[8,3,48,128]{3,2,1,0:T(8,128)S(1)}, f32[8,3,48,128]{3,2,1,0:T(8,128)}, u32[]{:S(2)}) copy-start(f32[8,3,48,128]{3,2,1,0:T(8,128)} %get-tuple-element.39) | copy-start | bytes 1769476
  49.7 13.7 %collective-permute-start.3 = (f32[8,3,48,128]{3,2,1,0:T(8,128)S(1)}, f32[8,3,48,128]{3,2,1,0:T(8,128)S(1)}, u32[]{:S(2)}, u32[]{:S(2)}) collective-permute-start(f32[8,3,48,128]{3,2,1,0:T(8,128)S(1)} %get-tuple-element.33), channel_id=1, source_target_pairs={{0,3},{1,0},{2,1},{3,2},{4,7},{5,4},{6,5},{7,6},{8,11},{9,8},{10,9... | collective-permute-start | bytes 1769480 | tf_op jit(solution)/shard_map/ppermute | solution.py:76
  63.7 8.4 %collective-permute-start.7 = (f32[2,6,48,128]{3,2,1,0:T(8,128)S(1)}, f32[2,6,48,128]{3,2,1,0:T(8,128)S(1)}, u32[]{:S(2)}, u32[]{:S(2)}) collective-permute-start(f32[2,6,48,128]{3,2,1,0:T(8,128)S(1)} %get-tuple-element.51), channel_id=1, source_target_pairs={{0,8},{1,9},{2,10},{3,11},{4,12},{5,13},{6,14},{7,15},{8,0},{9,1},... | collective-permute-start | bytes 884744 | tf_op jit(solution)/shard_map/ppermute | solution.py:76
  66.1 9.1 %collective-permute-start.8 = (f32[2,6,48,128]{3,2,1,0:T(8,128)S(1)}, f32[2,6,48,128]{3,2,1,0:T(8,128)S(1)}, u32[]{:S(2)}, u32[]{:S(2)}) collective-permute-start(f32[2,6,48,128]{3,2,1,0:T(8,128)S(1)} %get-tuple-element.53), channel_id=1, source_target_pairs={{0,4},{1,5},{2,6},{3,7},{4,8},{5,9},{6,10},{7,11},{8,12},{9,13},{1... | collective-permute-start | bytes 884744 | tf_op jit(solution)/shard_map/ppermute | solution.py:76
  66.5 8.6 %collective-permute-start.9 = (f32[2,6,48,128]{3,2,1,0:T(8,128)S(1)}, f32[2,6,48,128]{3,2,1,0:T(8,128)S(1)}, u32[]{:S(2)}, u32[]{:S(2)}) collective-permute-start(f32[2,6,48,128]{3,2,1,0:T(8,128)S(1)} %get-tuple-element.52), channel_id=1, source_target_pairs={{0,12},{1,13},{2,14},{3,15},{4,0},{5,1},{6,2},{7,3},{8,4},{9,5},{1... | collective-permute-start | bytes 884744 | tf_op jit(solution)/shard_map/ppermute | solution.py:76
  75.2 13.5 %collective-permute-start.10 = (f32[296,128]{1,0:T(8,128)S(1)}, f32[296,128]{1,0:T(8,128)S(1)}, u32[]{:S(2)}, u32[]{:S(2)}) collective-permute-start(f32[296,128]{1,0:T(8,128)S(1)} %get-tuple-element.54), channel_id=1, source_target_pairs={{0,64},{1,65},{2,66},{3,67},{4,68},{5,69},{6,70},{7,71},{8,72},{9,... | collective-permute-start | bytes 454664 | tf_op jit(solution)/shard_map/ppermute | solution.py:76
  78.0 13.9 %collective-permute-start.11 = (f32[296,128]{1,0:T(8,128)S(1)}, f32[296,128]{1,0:T(8,128)S(1)}, u32[]{:S(2)}, u32[]{:S(2)}) collective-permute-start(f32[296,128]{1,0:T(8,128)S(1)} %get-tuple-element.55), channel_id=1, source_target_pairs={{0,16},{1,17},{2,18},{3,19},{4,20},{5,21},{6,22},{7,23},{8,24},{9,... | collective-permute-start | bytes 454664 | tf_op jit(solution)/shard_map/ppermute | solution.py:76
  88.2 6.4 %collective-permute-start.12 = (f32[296,128]{1,0:T(8,128)S(1)}, f32[296,128]{1,0:T(8,128)S(1)}, u32[]{:S(2)}, u32[]{:S(2)}) collective-permute-start(f32[296,128]{1,0:T(8,128)S(1)} %get-tuple-element.55), channel_id=1, source_target_pairs={{0,80},{1,81},{2,82},{3,83},{4,84},{5,85},{6,86},{7,87},{8,88},{9,... | collective-permute-start | bytes 454664 | tf_op jit(solution)/shard_map/ppermute | solution.py:76
  94.6 8.9 %collective-permute-start.14 = (f32[192,128]{1,0:T(8,128)S(1)}, f32[192,128]{1,0:T(8,128)S(1)}, u32[]{:S(2)}, u32[]{:S(2)}) collective-permute-start(f32[192,128]{1,0:T(8,128)S(1)} %pad_maximum_fusion.5), channel_id=1, source_target_pairs={{0,1},{1,2},{2,3},{3,4},{4,5},{5,6},{6,7},{7,8},{8,9},{9,10},{10,1... | collective-permute-start | bytes 294920 | tf_op jit(solution)/shard_map/ppermute | solution.py:76
  95.1 9.4 %collective-permute-start.13 = (f32[96,128]{1,0:T(8,128)S(1)}, f32[96,128]{1,0:T(8,128)S(1)}, u32[]{:S(2)}, u32[]{:S(2)}) collective-permute-start(f32[96,128]{1,0:T(8,128)S(1)} %slice_select_fusion), channel_id=1, source_target_pairs={{0,2},{1,3},{2,4},{3,5},{4,6},{5,7},{6,8},{7,9},{8,10},{9,11},{10,... | collective-permute-start | bytes 147464 | tf_op jit(solution)/shard_map/ppermute | solution.py:76
  104.5 8.5 %collective-permute-start.15 = (f32[288,128]{1,0:T(8,128)S(1)}, f32[288,128]{1,0:T(8,128)S(1)}, u32[]{:S(2)}, u32[]{:S(2)}) collective-permute-start(f32[288,128]{1,0:T(8,128)S(1)} %pad_maximum_fusion.4), channel_id=1, source_target_pairs={{0,64},{1,65},{2,66},{3,67},{4,68},{5,69},{6,70},{7,71},{8,72},{9,... | collective-permute-start | bytes 442376 | tf_op jit(solution)/shard_map/ppermute | solution.py:76
  113.0 3.2 %collective-permute-start.16 = (f32[872,128]{1,0:T(8,128)S(1)}, f32[872,128]{1,0:T(8,128)S(1)}, u32[]{:S(2)}, u32[]{:S(2)}) collective-permute-start(f32[872,128]{1,0:T(8,128)S(1)} %pad_maximum_fusion), channel_id=1, source_target_pairs={{0,32},{1,33},{2,34},{3,35},{4,36},{5,37},{6,38},{7,39},{8,40},{9,... | collective-permute-start | bytes 1339400 | tf_op jit(solution)/shard_map/ppermute | solution.py:76
  113.1 2.0 %collective-permute-start.17 = (bf16[15,48,128]{2,1,0:T(8,128)(2,1)S(1)}, bf16[15,48,128]{2,1,0:T(8,128)(2,1)S(1)}, u32[]{:S(2)}, u32[]{:S(2)}) collective-permute-start(bf16[15,48,128]{2,1,0:T(8,128)(2,1)S(1)} %get-tuple-element.43.iown_ref), channel_id=1, source_target_pairs={{0,32},{1,33},{2,34},{3,35},{4,36},{5,37},{6,38},{7,39},{8,40},{9,... | collective-permute-start | bytes 552968 | tf_op jit(solution)/shard_map/ppermute | solution.py:76
where the time goes:
time: 134 us; the launch traced here: 133 us
  starting transfers between devices  50.7 us (38%)
  waiting for transfers between devices  35.8 us (27%)
  Pallas kernels  31.7 us (24%)
  blocking collectives  13.2 us (10%)
    ppermute x18, starting transfers between devices, permute(): return lax.ppermute(x, BOTH, table)  41.3 us
    ppermute x18, waiting for transfers between devices, permute(): return lax.ppermute(x, BOTH, table)  30.7 us
    all_to_all x1, blocking collectives, step(): lax.all_to_all(jnp.broadcast_to(stats[None], (32, 1, NY)), 'sub', 0, 0, t...  13.2 us
    pallas_call x1, Pallas kernels, moving_planes(): pl.pallas_call(moving_kernel, out_shape=[pltpu.HBM((4, PAGES, OWN, NY), F...  9.65 us
    all_to_all x1, starting transfers between devices, step(): image = lax.all_to_all(copies, 'sub', 0, 0, tiled=True).reshape(NZ, WIN, NY)  9.39 us
    pallas_call x1, Pallas kernels, template_planes(): pl.pallas_call(template_kernel, out_shape=[PLANES, RAW, jax.ShapeDtypeStr...  8.11 us
    pallas_call x4, Pallas kernels, factors(): pl.pallas_call(functools.partial(factor_kernel, kb), out_shape=[jax.Shape...  7.3 us
    all_to_all x1, waiting for transfers between devices, step(): image = lax.all_to_all(copies, 'sub', 0, 0, tiled=True).reshape(NZ, WIN, NY)  5.11 us
  transfers between devices with their start and end apart: 19, of which 11 were waited for; matrix products, arithmetic and copies ran while one was open for 0% of the time, Pallas kernels for 21%

commit v1 on v0

--- a/solution.py
+++ b/solution.py
@@ -297,29 +297,6 @@
 
 def in_vmem(x):
     return pltpu.with_memory_space_constraint(x, pltpu.VMEM)
-
-
-def window_kernel(core, template, out, held, sem):
-    rows = pl.ds(pl.multiple_of(core[0] * (NX - WIN), 8), WIN)
-    fetch = pltpu.make_async_copy(template.at[:, rows], held, sem)
-    fetch.start()
-    fetch.wait()
-    window = held[...]
-    for d in range(32):
-        out[d] = window
-
-
-def window_copies(core, template):
-    return pl.pallas_call(
-        window_kernel,
-        out_shape=pltpu.VMEM((32, 3, WIN, NY), BF16),
-        in_specs=[SMALL, FAR],
-        out_specs=NEAR,
-        scratch_shapes=[pltpu.VMEM((3, WIN, NY), BF16), pltpu.SemaphoreType.DMA],
-        compiler_params=pltpu.CompilerParams(vmem_limit_bytes=2 << 20),
-        cost_estimate=pl.CostEstimate(flops=1, bytes_accessed=10**6, transcendentals=0),
-        name="window_copies",
-    )(core, in_hbm(template))
 
 
 def moving_planes(idx, ja, jb):
@@ -675,7 +652,8 @@
 
     keep = subjects[0]
     take = permute(keep, CORE_PAIRS)
-    copies = window_copies(core.astype(jnp.int32).reshape(1), template)
+    mine = lax.dynamic_slice_in_dim(template, 40 * core, WIN, axis=1)
+    copies = jnp.broadcast_to(mine[None], (32, 3, WIN, NY))
     image = lax.all_to_all(copies, "sub", 0, 0, tiled=True).reshape(NZ, WIN, NY)
 
     jplane, *j_blocks = moving_planes(idx, keep, take)
@@ -707,8 +685,8 @@
         [f_half, jnp.where(low, m_half[2 * OWN :], m_half[:OWN])], axis=0
     )
     far = jnp.where(low, f_half[OWN:], f_half[: 2 * OWN])
+    far = permute(far, slab_shift(2))
     near = permute(near, slab_shift(1))
-    far = permute(far, slab_shift(2))
     near_f, near_m = near[: 3 * OWN], near[3 * OWN :]
     f_side = jnp.where(
         low, jnp.concatenate([far, near_f], axis=0), jnp.concatenate([near_f, far], axis=0)

time: 134 us -> 124 us (0.925)
  starting transfers between devices: 50.7 us -> 42.3 us
  waiting for transfers between devices: 35.8 us -> 33.4 us
  Pallas kernels: 31.7 us -> 29.6 us
  local copies, waits for them, and re-layouts: 0.12 us -> 2.16 us
    ppermute x18, starting transfers between devices: 41.3 us -> 32.9 us  [permute(): return lax.ppermute(x, BOTH, table)]
    pallas_call x1 -> x0, Pallas kernels: 2.07 us -> none  [window_copies(): pl.pallas_call(window_kernel, out_shape=pltpu.VMEM((32, 3, WIN, NY), BF16...]
    ppermute x18, waiting for transfers between devices: 30.7 us -> 28.7 us  [permute(): return lax.ppermute(x, BOTH, table)]
  transfers between devices with their start and end apart: 19 -> 19, of which waited for: 11 -> 11; matrix products, arithmetic and copies ran while one was open for 0% -> 1% of each run, Pallas kernels for 21% -> 21%
where the time goes in v1:
time: 124 us; the launch traced here: 122 us
  starting transfers between devices  42.3 us (34%)
  waiting for transfers between devices  33.4 us (27%)
  Pallas kernels  29.6 us (24%)
  blocking collectives  13.2 us (11%)
  local copies, waits for them, and re-layouts  2.16 us (2%)
    ppermute x18, starting transfers between devices, permute(): return lax.ppermute(x, BOTH, table)  32.9 us
    ppermute x18, waiting for transfers between devices, permute(): return lax.ppermute(x, BOTH, table)  28.7 us
    all_to_all x1, blocking collectives, step(): lax.all_to_all(jnp.broadcast_to(stats[None], (32, 1, NY)), 'sub', 0, 0, t...  13.2 us
    pallas_call x1, Pallas kernels, moving_planes(): pl.pallas_call(moving_kernel, out_shape=[pltpu.HBM((4, PAGES, OWN, NY), F...  9.67 us
    all_to_all x1, starting transfers between devices, step(): image = lax.all_to_all(copies, 'sub', 0, 0, tiled=True).reshape(NZ, WIN, NY)  9.37 us
    pallas_call x1, Pallas kernels, template_planes(): pl.pallas_call(template_kernel, out_shape=[PLANES, RAW, jax.ShapeDtypeStr...  8.1 us
    pallas_call x4, Pallas kernels, factors(): pl.pallas_call(functools.partial(factor_kernel, kb), out_shape=[jax.Shape...  7.3 us
    all_to_all x1, waiting for transfers between devices, step(): image = lax.all_to_all(copies, 'sub', 0, 0, tiled=True).reshape(NZ, WIN, NY)  4.68 us
  transfers between devices with their start and end apart: 19, of which 11 were waited for; matrix products, arithmetic and copies ran while one was open for 1% of the time, Pallas kernels for 21%

profile of v1, /device:TPU:0, one launch (start us, length us, event | category | flops | bytes accessed | tf_op | source)
XLA Modules:
  0.0 122.2 jit_solution(12816962536961425776)
XLA Ops:
  0.6 0.0 copy-start
  0.6 0.1 collective-permute-start
  0.8 0.8 copy-done
  1.5 1.3 %broadcast_in_dim.8 = bf16[32,3,56,128]{3,2,1,0:T(8,128)(2,1)} broadcast(bf16[3,56,128]{2,1,0:T(8,128)(2,1)S(1)} %constant_dynamic-slice_fusion), dimensions={1,2,3} | broadcast | bytes 1419264 | tf_op jit(solution)/shard_map/broadcast_in_dim | solution.py:656
  2.8 9.4 %all-to-all-start = ((bf16[32,3,56,128]{3,2,1,0:T(8,128)(2,1)}), bf16[32,3,56,128]{3,2,1,0:T(8,128)(2,1)S(1)}, u32[]{:S(2)}, u32[]{:S(2)}) async-start(bf16[32,3,56,128]{3,2,1,0:T(8,128)(2,1)} %broadcast_in_dim.8), calls=%async_computation | async-start | bytes 2752512 | tf_op jit(solution)/shard_map/all_to_all | solution.py:657
  12.2 0.1 stack.27.idx
  12.3 0.0 collective-permute-done.jb_hbm
  12.3 9.7 %moving_planes.1 = (f32[4,104,48,128]{3,2,1,0:T(8,128)}, f32[8,3,48,128]{3,2,1,0:T(8,128)}, f32[8,3,48,128]{3,2,1,0:T(8,128)}, f32[8,3,48,128]{3,2,1,0:T(8,128)}, f32[8,3,48,128]{3,2,1,0:T(8,128)}) custom-call(s32[6]{0:T(128)S(1)} %stack.27.idx, bf16[96,96,128]{2,1,0:T(8,128)(2,1)} %bitcast.24, bf16[96,96,128]{2,1,0:T(8,128)(2,1)} %collective-permute-done.jb_hbm), custom_call_target="tpu_custom_call" | custom-call | flops 4000000000 | bytes 6000000 | tf_op jit(solution)/shard_map/moving_planes/pallas_call | solution.py:303
  22.0 1.8 %collective-permute-start.4 = (f32[8,3,48,128]{3,2,1,0:T(8,128)}, f32[8,3,48,128]{3,2,1,0:T(8,128)S(1)}, u32[]{:S(2)}, u32[]{:S(2)}) collective-permute-start(f32[8,3,48,128]{3,2,1,0:T(8,128)} %get-tuple-element.40), channel_id=1, source_target_pairs={{0,1},{1,2},{2,3},{3,0},{4,5},{5,6},{6,7},{7,4},{8,9},{9,10},{10,1... | collective-permute-start | bytes 1769480 | tf_op jit(solution)/shard_map/ppermute | solution.py:76
  23.8 2.7 %collective-permute-start.5 = (f32[8,3,48,128]{3,2,1,0:T(8,128)}, f32[8,3,48,128]{3,2,1,0:T(8,128)S(1)}, u32[]{:S(2)}, u32[]{:S(2)}) collective-permute-start(f32[8,3,48,128]{3,2,1,0:T(8,128)} %get-tuple-element.41), channel_id=1, source_target_pairs={{0,2},{1,3},{2,0},{3,1},{4,6},{5,7},{6,4},{7,5},{8,10},{9,11},{10,... | collective-permute-start | bytes 1769480 | tf_op jit(solution)/shard_map/ppermute | solution.py:76
  26.5 1.5 %collective-permute-start.6 = (f32[8,3,48,128]{3,2,1,0:T(8,128)}, f32[8,3,48,128]{3,2,1,0:T(8,128)S(1)}, u32[]{:S(2)}, u32[]{:S(2)}) collective-permute-start(f32[8,3,48,128]{3,2,1,0:T(8,128)} %get-tuple-element.42), channel_id=1, source_target_pairs={{0,3},{1,0},{2,1},{3,2},{4,7},{5,4},{6,5},{7,6},{8,11},{9,8},{10,9... | collective-permute-start | bytes 1769480 | tf_op jit(solution)/shard_map/ppermute | solution.py:76
  28.0 4.7 %all-to-all-done = bf16[32,3,56,128]{3,2,1,0:T(8,128)(2,1)S(1)} async-done(((bf16[32,3,56,128]{3,2,1,0:T(8,128)(2,1)}), bf16[32,3,56,128]{3,2,1,0:T(8,128)(2,1)S(1)}, u32[]{:S(2)}, u32[]{:S(2)}) %all-to-all-start) | async-done | bytes 1376288 | tf_op jit(solution)/shard_map/all_to_all | solution.py:657
  32.7 0.0 copy-start.1
  32.7 8.1 %template_planes.1 = (f32[4,104,48,128]{3,2,1,0:T(8,128)S(1)}, f32[3,96,56,128]{3,2,1,0:T(8,128)S(1)}, bf16[15,48,128]{2,1,0:T(8,128)(2,1)S(1)}) custom-call(s32[6]{0:T(128)S(1)} %stack.27.idx, bf16[96,56,128]{2,1,0:T(8,128)(2,1)S(1)} %bitcast.18, bf16[96,96,128]{2,1,0:T(8,128)(2,1)} %bitcast.25, bf16[96,96,128]{2,1,0:T(8,128)(2,1)} %collective-permute-done.jb_hbm), custom_call_target="tpu_custom_call" | custom-call | flops 4000000000 | bytes 5000000 | tf_op jit(solution)/shard_map/template_planes/pallas_call | solution.py:370
  40.8 0.0 copy-done.1
  40.8 1.9 %factors.5 = (f32[8,3,48,128]{3,2,1,0:T(8,128)S(1)}, f32[8,128]{1,0:T(8,128)S(1)}) custom-call(s32[6]{0:T(128)S(1)} %stack.27.idx, f32[4,104,48,128]{3,2,1,0:T(8,128)S(1)} %get-tuple-element.27.iplane, f32[4,104,48,128]{3,2,1,0:T(8,128)S(1)} %copy-done.1, f32[3,96,56,128]{3,2,1,0:T(8,128)S(1)} %get-tuple-element.29.raw), custom_call_target="tpu_custom_call" | custom-call | flops 400000000 | bytes 1000000 | tf_op jit(solution)/shard_map/factors/pallas_call | solution.py:431
  42.7 1.1 collective-permute-start.1
  43.7 1.8 %factors.6 = (f32[8,3,48,128]{3,2,1,0:T(8,128)S(1)}, f32[8,128]{1,0:T(8,128)S(1)}) custom-call(s32[6]{0:T(128)S(1)} %stack.27.idx, f32[4,104,48,128]{3,2,1,0:T(8,128)S(1)} %get-tuple-element.27.iplane, f32[4,104,48,128]{3,2,1,0:T(8,128)S(1)} %copy-done.1, f32[3,96,56,128]{3,2,1,0:T(8,128)S(1)} %get-tuple-element.29.raw), custom_call_target="tpu_custom_call" | custom-call | flops 400000000 | bytes 1000000 | tf_op jit(solution)/shard_map/factors/pallas_call | solution.py:431
  45.6 1.8 %collective-permute-start.2 = (f32[8,3,48,128]{3,2,1,0:T(8,128)S(1)}, f32[8,3,48,128]{3,2,1,0:T(8,128)S(1)}, u32[]{:S(2)}, u32[]{:S(2)}) collective-permute-start(f32[8,3,48,128]{3,2,1,0:T(8,128)S(1)} %get-tuple-element.32), channel_id=1, source_target_pairs={{0,2},{1,3},{2,0},{3,1},{4,6},{5,7},{6,4},{7,5},{8,10},{9,11},{10,... | collective-permute-start | bytes 1769480 | tf_op jit(solution)/shard_map/ppermute | solution.py:76
  47.4 1.8 %factors.7 = (f32[8,3,48,128]{3,2,1,0:T(8,128)S(1)}, f32[8,128]{1,0:T(8,128)S(1)}) custom-call(s32[6]{0:T(128)S(1)} %stack.27.idx, f32[4,104,48,128]{3,2,1,0:T(8,128)S(1)} %get-tuple-element.27.iplane, f32[4,104,48,128]{3,2,1,0:T(8,128)S(1)} %copy-done.1, f32[3,96,56,128]{3,2,1,0:T(8,128)S(1)} %get-tuple-element.29.raw), custom_call_target="tpu_custom_call" | custom-call | flops 400000000 | bytes 1000000 | tf_op jit(solution)/shard_map/factors/pallas_call | solution.py:431
  49.1 0.0 collective-permute-done.4
  49.1 0.0 copy-start.2
  49.2 1.8 %collective-permute-start.3 = (f32[8,3,48,128]{3,2,1,0:T(8,128)S(1)}, f32[8,3,48,128]{3,2,1,0:T(8,128)S(1)}, u32[]{:S(2)}, u32[]{:S(2)}) collective-permute-start(f32[8,3,48,128]{3,2,1,0:T(8,128)S(1)} %get-tuple-element.33), channel_id=1, source_target_pairs={{0,3},{1,0},{2,1},{3,2},{4,7},{5,4},{6,5},{7,6},{8,11},{9,8},{10,9... | collective-permute-start | bytes 1769480 | tf_op jit(solution)/shard_map/ppermute | solution.py:76
  50.9 1.8 %factors.4 = (f32[8,3,48,128]{3,2,1,0:T(8,128)S(1)}, f32[8,128]{1,0:T(8,128)S(1)}) custom-call(s32[6]{0:T(128)S(1)} %stack.27.idx, f32[4,104,48,128]{3,2,1,0:T(8,128)S(1)} %get-tuple-element.27.iplane, f32[4,104,48,128]{3,2,1,0:T(8,128)S(1)} %copy-done.1, f32[3,96,56,128]{3,2,1,0:T(8,128)S(1)} %get-tuple-element.29.raw), custom_call_target="tpu_custom_call" | custom-call | flops 400000000 | bytes 1000000 | tf_op jit(solution)/shard_map/factors/pallas_call | solution.py:431
  52.8 0.0 collective-permute-done.5
  52.8 0.0 collective-permute-done.6
  52.8 0.0 copy-done.2
  52.8 0.1 add_add_fusion
  52.9 7.2 %collective-permute-done.1 = f32[8,3,48,128]{3,2,1,0:T(8,128)S(1)} collective-permute-done((f32[8,3,48,128]{3,2,1,0:T(8,128)S(1)}, f32[8,3,48,128]{3,2,1,0:T(8,128)S(1)}, u32[]{:S(2)}, u32[]{:S(2)}) %collective-permute-start.1) | collective-permute-done | bytes 589856 | tf_op jit(solution)/shard_map/ppermute | solution.py:76
  60.1 0.0 collective-permute-done.2
  60.1 2.8 %collective-permute-done.3 = f32[8,3,48,128]{3,2,1,0:T(8,128)S(1)} collective-permute-done((f32[8,3,48,128]{3,2,1,0:T(8,128)S(1)}, f32[8,3,48,128]{3,2,1,0:T(8,128)S(1)}, u32[]{:S(2)}, u32[]{:S(2)}) %collective-permute-start.3) | collective-permute-done | bytes 589856 | tf_op jit(solution)/shard_map/ppermute | solution.py:76
  63.0 0.2 add_add_fusion.1
  63.1 0.1 fusion.5
  63.2 3.4 %collective-permute-start.7 = (f32[2,6,48,128]{3,2,1,0:T(8,128)S(1)}, f32[2,6,48,128]{3,2,1,0:T(8,128)S(1)}, u32[]{:S(2)}, u32[]{:S(2)}) collective-permute-start(f32[2,6,48,128]{3,2,1,0:T(8,128)S(1)} %get-tuple-element.51), channel_id=1, source_target_pairs={{0,8},{1,9},{2,10},{3,11},{4,12},{5,13},{6,14},{7,15},{8,0},{9,1},... | collective-permute-start | bytes 884744 | tf_op jit(solution)/shard_map/ppermute | solution.py:76
  66.6 0.0 collective-permute-start.8
  66.6 3.2 %collective-permute-start.9 = (f32[2,6,48,128]{3,2,1,0:T(8,128)S(1)}, f32[2,6,48,128]{3,2,1,0:T(8,128)S(1)}, u32[]{:S(2)}, u32[]{:S(2)}) collective-permute-start(f32[2,6,48,128]{3,2,1,0:T(8,128)S(1)} %get-tuple-element.52), channel_id=1, source_target_pairs={{0,12},{1,13},{2,14},{3,15},{4,0},{5,1},{6,2},{7,3},{8,4},{9,5},{1... | collective-permute-start | bytes 884744 | tf_op jit(solution)/shard_map/ppermute | solution.py:76
  69.8 1.7 %collective-permute-done.7 = f32[2,6,48,128]{3,2,1,0:T(8,128)S(1)} collective-permute-done((f32[2,6,48,128]{3,2,1,0:T(8,128)S(1)}, f32[2,6,48,128]{3,2,1,0:T(8,128)S(1)}, u32[]{:S(2)}, u32[]{:S(2)}) %collective-permute-start.7) | collective-permute-done | bytes 294944 | tf_op jit(solution)/shard_map/ppermute | solution.py:76
  71.5 3.1 %collective-permute-done.8 = f32[2,6,48,128]{3,2,1,0:T(8,128)S(1)} collective-permute-done((f32[2,6,48,128]{3,2,1,0:T(8,128)S(1)}, f32[2,6,48,128]{3,2,1,0:T(8,128)S(1)}, u32[]{:S(2)}, u32[]{:S(2)}) %collective-permute-start.8) | collective-permute-done | bytes 294944 | tf_op jit(solution)/shard_map/ppermute | solution.py:76
  74.7 0.0 collective-permute-done.9
  74.7 0.1 fusion.4
  74.8 2.8 %collective-permute-start.10 = (f32[296,128]{1,0:T(8,128)S(1)}, f32[296,128]{1,0:T(8,128)S(1)}, u32[]{:S(2)}, u32[]{:S(2)}) collective-permute-start(f32[296,128]{1,0:T(8,128)S(1)} %get-tuple-element.54), channel_id=1, source_target_pairs={{0,64},{1,65},{2,66},{3,67},{4,68},{5,69},{6,70},{7,71},{8,72},{9,... | collective-permute-start | bytes 454664 | tf_op jit(solution)/shard_map/ppermute | solution.py:76
  77.6 0.2 collective-permute-start.11
  77.8 3.1 %collective-permute-start.12 = (f32[296,128]{1,0:T(8,128)S(1)}, f32[296,128]{1,0:T(8,128)S(1)}, u32[]{:S(2)}, u32[]{:S(2)}) collective-permute-start(f32[296,128]{1,0:T(8,128)S(1)} %get-tuple-element.55), channel_id=1, source_target_pairs={{0,80},{1,81},{2,82},{3,83},{4,84},{5,85},{6,86},{7,87},{8,88},{9,... | collective-permute-start | bytes 454664 | tf_op jit(solution)/shard_map/ppermute | solution.py:76
  80.8 0.7 collective-permute-done.10
  81.6 2.4 %collective-permute-done.11 = f32[296,128]{1,0:T(8,128)S(1)} collective-permute-done((f32[296,128]{1,0:T(8,128)S(1)}, f32[296,128]{1,0:T(8,128)S(1)}, u32[]{:S(2)}, u32[]{:S(2)}) %collective-permute-start.11) | collective-permute-done | bytes 151584 | tf_op jit(solution)/shard_map/ppermute | solution.py:76
  84.0 0.0 collective-permute-done.12
  84.1 1.1 collective-permute-start.14
  85.2 3.0 %collective-permute-start.13 = (f32[96,128]{1,0:T(8,128)S(1)}, f32[96,128]{1,0:T(8,128)S(1)}, u32[]{:S(2)}, u32[]{:S(2)}) collective-permute-start(f32[96,128]{1,0:T(8,128)S(1)} %slice_select_fusion), channel_id=1, source_target_pairs={{0,2},{1,3},{2,4},{3,5},{4,6},{5,7},{6,8},{7,9},{8,10},{9,11},{10,... | collective-permute-start | bytes 147464 | tf_op jit(solution)/shard_map/ppermute | solution.py:76
  88.3 5.0 %collective-permute-done.14 = f32[192,128]{1,0:T(8,128)S(1)} collective-permute-done((f32[192,128]{1,0:T(8,128)S(1)}, f32[192,128]{1,0:T(8,128)S(1)}, u32[]{:S(2)}, u32[]{:S(2)}) %collective-permute-start.14) | collective-permute-done | bytes 98336 | tf_op jit(solution)/shard_map/ppermute | solution.py:76
  93.3 0.9 collective-permute-done.13
  94.2 4.8 %collective-permute-start.15 = (f32[288,128]{1,0:T(8,128)S(1)}, f32[288,128]{1,0:T(8,128)S(1)}, u32[]{:S(2)}, u32[]{:S(2)}) collective-permute-start(f32[288,128]{1,0:T(8,128)S(1)} %pad_maximum_fusion.4), channel_id=1, source_target_pairs={{0,64},{1,65},{2,66},{3,67},{4,68},{5,69},{6,70},{7,71},{8,72},{9,... | collective-permute-start | bytes 442376 | tf_op jit(solution)/shard_map/ppermute | solution.py:76
  99.1 3.1 %collective-permute-done.15.twin_ref = f32[288,128]{1,0:T(8,128)S(1)} collective-permute-done((f32[288,128]{1,0:T(8,128)S(1)}, f32[288,128]{1,0:T(8,128)S(1)}, u32[]{:S(2)}, u32[]{:S(2)}) %collective-permute-start.15) | collective-permute-done | bytes 147488 | tf_op jit(solution)/shard_map/ppermute | solution.py:76
  102.2 0.1 collective-permute-start.16
  102.3 0.5 collective-permute-start.17
  102.8 1.6 %collective-permute-done.17.iother_ref = bf16[15,48,128]{2,1,0:T(8,128)(2,1)S(1)} collective-permute-done((bf16[15,48,128]{2,1,0:T(8,128)(2,1)S(1)}, bf16[15,48,128]{2,1,0:T(8,128)(2,1)S(1)}, u32[]{:S(2)}, u32[]{:S(2)}) %collective-permute-start.17) | collective-permute-done | bytes 184352 | tf_op jit(solution)/shard_map/ppermute | solution.py:76
  104.4 1.0 slopes.1.slope_ref
  105.4 0.0 collective-permute-done.16.other_ref
  105.4 2.6 %smooth_slab.1 = (f32[3,3,96,128]{3,2,1,0:T(8,128)S(1)}, f32[3,96,128]{2,1,0:T(8,128)S(1)}, f32[3,96,128]{2,1,0:T(8,128)S(1)}, f32[1,128]{1,0:T(1,128)S(1)}) custom-call(s32[6]{0:T(128)S(1)} %stack.27.idx, f32[584,128]{1,0:T(8,128)S(1)} %pad_maximum_fusion.1.own_ref, f32[288,128]{1,0:T(8,128)S(1)} %collective-permute-done.15.twin_ref, ...), custom_call_target="tpu_custom_call" | custom-call | flops 100000000 | bytes 3000000 | tf_op jit(solution)/shard_map/smooth_slab/pallas_call | solution.py:579
  108.1 13.2 %all_to_all.10 = f32[32,1,128]{2,1,0:T(1,128)S(1)} all-to-all(f32[32,1,128]{2,1,0:T(1,128)S(1)} %broadcast_in_dim.11), channel_id=1, replica_groups=mesh['grp'=4,'sub'=32] {'sub'}, dimensions={0} | all-to-all | bytes 32768 | tf_op jit(solution)/shard_map/all_to_all | solution.py:699
  121.3 0.9 finish.1
  (16 shorter events, 0.2 us)
Async XLA Ops:
  0.6 0.9 copy-start
  0.6 11.7 %collective-permute-start = (bf16[96,96,128]{2,1,0:T(8,128)(2,1)}, bf16[96,96,128]{2,1,0:T(8,128)(2,1)}, u32[]{:S(2)}, u32[]{:S(2)}) collective-permute-start(bf16[96,96,128]{2,1,0:T(8,128)(2,1)} %bitcast.23), channel_id=1, source_target_pairs={{0,32},{1,33},{2,34},{3,35},{4,36},{5,37},{6,38},{7,39},{8,40},{9,... | collective-permute-start | bytes 7077896 | tf_op jit(solution)/shard_map/ppermute | solution.py:76
  2.8 29.9 %all-to-all-start = ((bf16[32,3,56,128]{3,2,1,0:T(8,128)(2,1)}), bf16[32,3,56,128]{3,2,1,0:T(8,128)(2,1)S(1)}, u32[]{:S(2)}, u32[]{:S(2)}) async-start(bf16[32,3,56,128]{3,2,1,0:T(8,128)(2,1)} %broadcast_in_dim.8), calls=%async_computation | async-start | bytes 2752512 | tf_op jit(solution)/shard_map/all_to_all | solution.py:657
  22.0 27.1 %collective-permute-start.4 = (f32[8,3,48,128]{3,2,1,0:T(8,128)}, f32[8,3,48,128]{3,2,1,0:T(8,128)S(1)}, u32[]{:S(2)}, u32[]{:S(2)}) collective-permute-start(f32[8,3,48,128]{3,2,1,0:T(8,128)} %get-tuple-element.40), channel_id=1, source_target_pairs={{0,1},{1,2},{2,3},{3,0},{4,5},{5,6},{6,7},{7,4},{8,9},{9,10},{10,1... | collective-permute-start | bytes 1769480 | tf_op jit(solution)/shard_map/ppermute | solution.py:76
  23.8 28.9 %collective-permute-start.5 = (f32[8,3,48,128]{3,2,1,0:T(8,128)}, f32[8,3,48,128]{3,2,1,0:T(8,128)S(1)}, u32[]{:S(2)}, u32[]{:S(2)}) collective-permute-start(f32[8,3,48,128]{3,2,1,0:T(8,128)} %get-tuple-element.41), channel_id=1, source_target_pairs={{0,2},{1,3},{2,0},{3,1},{4,6},{5,7},{6,4},{7,5},{8,10},{9,11},{10,... | collective-permute-start | bytes 1769480 | tf_op jit(solution)/shard_map/ppermute | solution.py:76
  26.5 26.3 %collective-permute-start.6 = (f32[8,3,48,128]{3,2,1,0:T(8,128)}, f32[8,3,48,128]{3,2,1,0:T(8,128)S(1)}, u32[]{:S(2)}, u32[]{:S(2)}) collective-permute-start(f32[8,3,48,128]{3,2,1,0:T(8,128)} %get-tuple-element.42), channel_id=1, source_target_pairs={{0,3},{1,0},{2,1},{3,2},{4,7},{5,4},{6,5},{7,6},{8,11},{9,8},{10,9... | collective-permute-start | bytes 1769480 | tf_op jit(solution)/shard_map/ppermute | solution.py:76
  32.7 8.1 %copy-start.1 = (f32[4,104,48,128]{3,2,1,0:T(8,128)S(1)}, f32[4,104,48,128]{3,2,1,0:T(8,128)}, u32[]{:S(2)}) copy-start(f32[4,104,48,128]{3,2,1,0:T(8,128)} %get-tuple-element.28.jplane) | copy-start | bytes 30670852
  42.7 17.5 %collective-permute-start.1 = (f32[8,3,48,128]{3,2,1,0:T(8,128)S(1)}, f32[8,3,48,128]{3,2,1,0:T(8,128)S(1)}, u32[]{:S(2)}, u32[]{:S(2)}) collective-permute-start(f32[8,3,48,128]{3,2,1,0:T(8,128)S(1)} %get-tuple-element.31), channel_id=1, source_target_pairs={{0,1},{1,2},{2,3},{3,0},{4,5},{5,6},{6,7},{7,4},{8,9},{9,10},{10,1... | collective-permute-start | bytes 1769480 | tf_op jit(solution)/shard_map/ppermute | solution.py:76
  45.6 14.6 %collective-permute-start.2 = (f32[8,3,48,128]{3,2,1,0:T(8,128)S(1)}, f32[8,3,48,128]{3,2,1,0:T(8,128)S(1)}, u32[]{:S(2)}, u32[]{:S(2)}) collective-permute-start(f32[8,3,48,128]{3,2,1,0:T(8,128)S(1)} %get-tuple-element.32), channel_id=1, source_target_pairs={{0,2},{1,3},{2,0},{3,1},{4,6},{5,7},{6,4},{7,5},{8,10},{9,11},{10,... | collective-permute-start | bytes 1769480 | tf_op jit(solution)/shard_map/ppermute | solution.py:76
  49.1 3.6 %copy-start.2 = (f32[8,3,48,128]{3,2,1,0:T(8,128)S(1)}, f32[8,3,48,128]{3,2,1,0:T(8,128)}, u32[]{:S(2)}) copy-start(f32[8,3,48,128]{3,2,1,0:T(8,128)} %get-tuple-element.39) | copy-start | bytes 1769476
  49.2 13.8 %collective-permute-start.3 = (f32[8,3,48,128]{3,2,1,0:T(8,128)S(1)}, f32[8,3,48,128]{3,2,1,0:T(8,128)S(1)}, u32[]{:S(2)}, u32[]{:S(2)}) collective-permute-start(f32[8,3,48,128]{3,2,1,0:T(8,128)S(1)} %get-tuple-element.33), channel_id=1, source_target_pairs={{0,3},{1,0},{2,1},{3,2},{4,7},{5,4},{6,5},{7,6},{8,11},{9,8},{10,9... | collective-permute-start | bytes 1769480 | tf_op jit(solution)/shard_map/ppermute | solution.py:76
  63.2 8.3 %collective-permute-start.7 = (f32[2,6,48,128]{3,2,1,0:T(8,128)S(1)}, f32[2,6,48,128]{3,2,1,0:T(8,128)S(1)}, u32[]{:S(2)}, u32[]{:S(2)}) collective-permute-start(f32[2,6,48,128]{3,2,1,0:T(8,128)S(1)} %get-tuple-element.51), channel_id=1, source_target_pairs={{0,8},{1,9},{2,10},{3,11},{4,12},{5,13},{6,14},{7,15},{8,0},{9,1},... | collective-permute-start | bytes 884744 | tf_op jit(solution)/shard_map/ppermute | solution.py:76
  66.6 8.1 %collective-permute-start.8 = (f32[2,6,48,128]{3,2,1,0:T(8,128)S(1)}, f32[2,6,48,128]{3,2,1,0:T(8,128)S(1)}, u32[]{:S(2)}, u32[]{:S(2)}) collective-permute-start(f32[2,6,48,128]{3,2,1,0:T(8,128)S(1)} %get-tuple-element.53), channel_id=1, source_target_pairs={{0,4},{1,5},{2,6},{3,7},{4,8},{5,9},{6,10},{7,11},{8,12},{9,13},{1... | collective-permute-start | bytes 884744 | tf_op jit(solution)/shard_map/ppermute | solution.py:76
  66.6 8.1 %collective-permute-start.9 = (f32[2,6,48,128]{3,2,1,0:T(8,128)S(1)}, f32[2,6,48,128]{3,2,1,0:T(8,128)S(1)}, u32[]{:S(2)}, u32[]{:S(2)}) collective-permute-start(f32[2,6,48,128]{3,2,1,0:T(8,128)S(1)} %get-tuple-element.52), channel_id=1, source_target_pairs={{0,12},{1,13},{2,14},{3,15},{4,0},{5,1},{6,2},{7,3},{8,4},{9,5},{1... | collective-permute-start | bytes 884744 | tf_op jit(solution)/shard_map/ppermute | solution.py:76
  74.8 6.8 %collective-permute-start.10 = (f32[296,128]{1,0:T(8,128)S(1)}, f32[296,128]{1,0:T(8,128)S(1)}, u32[]{:S(2)}, u32[]{:S(2)}) collective-permute-start(f32[296,128]{1,0:T(8,128)S(1)} %get-tuple-element.54), channel_id=1, source_target_pairs={{0,64},{1,65},{2,66},{3,67},{4,68},{5,69},{6,70},{7,71},{8,72},{9,... | collective-permute-start | bytes 454664 | tf_op jit(solution)/shard_map/ppermute | solution.py:76
  77.6 6.4 %collective-permute-start.11 = (f32[296,128]{1,0:T(8,128)S(1)}, f32[296,128]{1,0:T(8,128)S(1)}, u32[]{:S(2)}, u32[]{:S(2)}) collective-permute-start(f32[296,128]{1,0:T(8,128)S(1)} %get-tuple-element.55), channel_id=1, source_target_pairs={{0,16},{1,17},{2,18},{3,19},{4,20},{5,21},{6,22},{7,23},{8,24},{9,... | collective-permute-start | bytes 454664 | tf_op jit(solution)/shard_map/ppermute | solution.py:76
  77.8 6.2 %collective-permute-start.12 = (f32[296,128]{1,0:T(8,128)S(1)}, f32[296,128]{1,0:T(8,128)S(1)}, u32[]{:S(2)}, u32[]{:S(2)}) collective-permute-start(f32[296,128]{1,0:T(8,128)S(1)} %get-tuple-element.55), channel_id=1, source_target_pairs={{0,80},{1,81},{2,82},{3,83},{4,84},{5,85},{6,86},{7,87},{8,88},{9,... | collective-permute-start | bytes 454664 | tf_op jit(solution)/shard_map/ppermute | solution.py:76
  84.1 9.2 %collective-permute-start.14 = (f32[192,128]{1,0:T(8,128)S(1)}, f32[192,128]{1,0:T(8,128)S(1)}, u32[]{:S(2)}, u32[]{:S(2)}) collective-permute-start(f32[192,128]{1,0:T(8,128)S(1)} %pad_maximum_fusion.5), channel_id=1, source_target_pairs={{0,1},{1,2},{2,3},{3,4},{4,5},{5,6},{6,7},{7,8},{8,9},{9,10},{10,1... | collective-permute-start | bytes 294920 | tf_op jit(solution)/shard_map/ppermute | solution.py:76
  85.2 9.0 %collective-permute-start.13 = (f32[96,128]{1,0:T(8,128)S(1)}, f32[96,128]{1,0:T(8,128)S(1)}, u32[]{:S(2)}, u32[]{:S(2)}) collective-permute-start(f32[96,128]{1,0:T(8,128)S(1)} %slice_select_fusion), channel_id=1, source_target_pairs={{0,2},{1,3},{2,4},{3,5},{4,6},{5,7},{6,8},{7,9},{8,10},{9,11},{10,... | collective-permute-start | bytes 147464 | tf_op jit(solution)/shard_map/ppermute | solution.py:76
  94.2 8.0 %collective-permute-start.15 = (f32[288,128]{1,0:T(8,128)S(1)}, f32[288,128]{1,0:T(8,128)S(1)}, u32[]{:S(2)}, u32[]{:S(2)}) collective-permute-start(f32[288,128]{1,0:T(8,128)S(1)} %pad_maximum_fusion.4), channel_id=1, source_target_pairs={{0,64},{1,65},{2,66},{3,67},{4,68},{5,69},{6,70},{7,71},{8,72},{9,... | collective-permute-start | bytes 442376 | tf_op jit(solution)/shard_map/ppermute | solution.py:76
  102.2 3.2 %collective-permute-start.16 = (f32[872,128]{1,0:T(8,128)S(1)}, f32[872,128]{1,0:T(8,128)S(1)}, u32[]{:S(2)}, u32[]{:S(2)}) collective-permute-start(f32[872,128]{1,0:T(8,128)S(1)} %pad_maximum_fusion), channel_id=1, source_target_pairs={{0,32},{1,33},{2,34},{3,35},{4,36},{5,37},{6,38},{7,39},{8,40},{9,... | collective-permute-start | bytes 1339400 | tf_op jit(solution)/shard_map/ppermute | solution.py:76
  102.3 2.0 %collective-permute-start.17 = (bf16[15,48,128]{2,1,0:T(8,128)(2,1)S(1)}, bf16[15,48,128]{2,1,0:T(8,128)(2,1)S(1)}, u32[]{:S(2)}, u32[]{:S(2)}) collective-permute-start(bf16[15,48,128]{2,1,0:T(8,128)(2,1)S(1)} %get-tuple-element.43.iown_ref), channel_id=1, source_target_pairs={{0,32},{1,33},{2,34},{3,35},{4,36},{5,37},{6,38},{7,39},{8,40},{9,... | collective-permute-start | bytes 552968 | tf_op jit(solution)/shard_map/ppermute | solution.py:76

commit v2 on v1

--- a/solution.py
+++ b/solution.py
@@ -630,7 +630,10 @@
 
 
 def round_one(blocks):
-    return [permute(blocks[k], first_round(k)) for k in (1, 2, 3)]
+    got = []
+    for k in (1, 3, 2):
+        got.append(permute(blocks[k], first_round(k)))
+    return got
 
 
 def round_two(total):
@@ -685,8 +688,8 @@
         [f_half, jnp.where(low, m_half[2 * OWN :], m_half[:OWN])], axis=0
     )
     far = jnp.where(low, f_half[OWN:], f_half[: 2 * OWN])
+    near = permute(near, slab_shift(1))
     far = permute(far, slab_shift(2))
-    near = permute(near, slab_shift(1))
     near_f, near_m = near[: 3 * OWN], near[3 * OWN :]
     f_side = jnp.where(
         low, jnp.concatenate([far, near_f], axis=0), jnp.concatenate([near_f, far], axis=0)

time: 124 us -> 124 us (level)
  no operation moved by 1% of the time
where the time goes in v2:
time: 124 us; the launch traced here: 122 us
  starting transfers between devices  41.7 us (34%)
  waiting for transfers between devices  34 us (27%)
  Pallas kernels  29.6 us (24%)
  blocking collectives  13.2 us (11%)
  local copies, waits for them, and re-layouts  2.16 us (2%)
    ppermute x18, starting transfers between devices, permute(): return lax.ppermute(x, BOTH, table)  32.3 us
    ppermute x18, waiting for transfers between devices, permute(): return lax.ppermute(x, BOTH, table)  28.7 us
    all_to_all x1, blocking collectives, step(): lax.all_to_all(jnp.broadcast_to(stats[None], (32, 1, NY)), 'sub', 0, 0, t...  13.2 us
    pallas_call x1, Pallas kernels, moving_planes(): pl.pallas_call(moving_kernel, out_shape=[pltpu.HBM((4, PAGES, OWN, NY), F...  9.67 us
    all_to_all x1, starting transfers between devices, step(): image = lax.all_to_all(copies, 'sub', 0, 0, tiled=True).reshape(NZ, WIN, NY)  9.37 us
    pallas_call x1, Pallas kernels, template_planes(): pl.pallas_call(template_kernel, out_shape=[PLANES, RAW, jax.ShapeDtypeStr...  8.1 us
    pallas_call x4, Pallas kernels, factors(): pl.pallas_call(functools.partial(factor_kernel, kb), out_shape=[jax.Shape...  7.3 us
    all_to_all x1, waiting for transfers between devices, step(): image = lax.all_to_all(copies, 'sub', 0, 0, tiled=True).reshape(NZ, WIN, NY)  5.29 us
  transfers between devices with their start and end apart: 19, of which 11 were waited for; matrix products, arithmetic and copies ran while one was open for 1% of the time, Pallas kernels for 21%

profile of v2, /device:TPU:0, one launch (start us, length us, event | category | flops | bytes accessed | tf_op | source)
XLA Modules:
  0.0 122.2 jit_solution(16082699077142576577)
XLA Ops:
  0.6 0.0 copy-start
  0.6 0.1 collective-permute-start
  0.8 0.8 copy-done
  1.5 1.3 %broadcast_in_dim.8 = bf16[32,3,56,128]{3,2,1,0:T(8,128)(2,1)} broadcast(bf16[3,56,128]{2,1,0:T(8,128)(2,1)S(1)} %constant_dynamic-slice_fusion), dimensions={1,2,3} | broadcast | bytes 1419264 | tf_op jit(solution)/shard_map/broadcast_in_dim | solution.py:659
  2.8 9.4 %all-to-all-start = ((bf16[32,3,56,128]{3,2,1,0:T(8,128)(2,1)}), bf16[32,3,56,128]{3,2,1,0:T(8,128)(2,1)S(1)}, u32[]{:S(2)}, u32[]{:S(2)}) async-start(bf16[32,3,56,128]{3,2,1,0:T(8,128)(2,1)} %broadcast_in_dim.8), calls=%async_computation | async-start | bytes 2752512 | tf_op jit(solution)/shard_map/all_to_all | solution.py:660
  12.2 0.1 stack.27.idx
  12.3 0.0 collective-permute-done.jb_hbm
  12.3 9.7 %moving_planes.1 = (f32[4,104,48,128]{3,2,1,0:T(8,128)}, f32[8,3,48,128]{3,2,1,0:T(8,128)}, f32[8,3,48,128]{3,2,1,0:T(8,128)}, f32[8,3,48,128]{3,2,1,0:T(8,128)}, f32[8,3,48,128]{3,2,1,0:T(8,128)}) custom-call(s32[6]{0:T(128)S(1)} %stack.27.idx, bf16[96,96,128]{2,1,0:T(8,128)(2,1)} %bitcast.24, bf16[96,96,128]{2,1,0:T(8,128)(2,1)} %collective-permute-done.jb_hbm), custom_call_target="tpu_custom_call" | custom-call | flops 4000000000 | bytes 6000000 | tf_op jit(solution)/shard_map/moving_planes/pallas_call | solution.py:303
  22.0 1.8 %collective-permute-start.4 = (f32[8,3,48,128]{3,2,1,0:T(8,128)}, f32[8,3,48,128]{3,2,1,0:T(8,128)S(1)}, u32[]{:S(2)}, u32[]{:S(2)}) collective-permute-start(f32[8,3,48,128]{3,2,1,0:T(8,128)} %get-tuple-element.40), channel_id=1, source_target_pairs={{0,1},{1,2},{2,3},{3,0},{4,5},{5,6},{6,7},{7,4},{8,9},{9,10},{10,1... | collective-permute-start | bytes 1769480 | tf_op jit(solution)/shard_map/ppermute | solution.py:76
  23.8 1.5 %collective-permute-start.5 = (f32[8,3,48,128]{3,2,1,0:T(8,128)}, f32[8,3,48,128]{3,2,1,0:T(8,128)S(1)}, u32[]{:S(2)}, u32[]{:S(2)}) collective-permute-start(f32[8,3,48,128]{3,2,1,0:T(8,128)} %get-tuple-element.41), channel_id=1, source_target_pairs={{0,3},{1,0},{2,1},{3,2},{4,7},{5,4},{6,5},{7,6},{8,11},{9,8},{10,9... | collective-permute-start | bytes 1769480 | tf_op jit(solution)/shard_map/ppermute | solution.py:76
  25.3 2.1 %collective-permute-start.6 = (f32[8,3,48,128]{3,2,1,0:T(8,128)}, f32[8,3,48,128]{3,2,1,0:T(8,128)S(1)}, u32[]{:S(2)}, u32[]{:S(2)}) collective-permute-start(f32[8,3,48,128]{3,2,1,0:T(8,128)} %get-tuple-element.42), channel_id=1, source_target_pairs={{0,2},{1,3},{2,0},{3,1},{4,6},{5,7},{6,4},{7,5},{8,10},{9,11},{10,... | collective-permute-start | bytes 1769480 | tf_op jit(solution)/shard_map/ppermute | solution.py:76
  27.4 5.3 %all-to-all-done = bf16[32,3,56,128]{3,2,1,0:T(8,128)(2,1)S(1)} async-done(((bf16[32,3,56,128]{3,2,1,0:T(8,128)(2,1)}), bf16[32,3,56,128]{3,2,1,0:T(8,128)(2,1)S(1)}, u32[]{:S(2)}, u32[]{:S(2)}) %all-to-all-start) | async-done | bytes 1376288 | tf_op jit(solution)/shard_map/all_to_all | solution.py:660
  32.7 0.0 copy-start.1
  32.7 8.1 %template_planes.1 = (f32[4,104,48,128]{3,2,1,0:T(8,128)S(1)}, f32[3,96,56,128]{3,2,1,0:T(8,128)S(1)}, bf16[15,48,128]{2,1,0:T(8,128)(2,1)S(1)}) custom-call(s32[6]{0:T(128)S(1)} %stack.27.idx, bf16[96,56,128]{2,1,0:T(8,128)(2,1)S(1)} %bitcast.18, bf16[96,96,128]{2,1,0:T(8,128)(2,1)} %bitcast.25, bf16[96,96,128]{2,1,0:T(8,128)(2,1)} %collective-permute-done.jb_hbm), custom_call_target="tpu_custom_call" | custom-call | flops 4000000000 | bytes 5000000 | tf_op jit(solution)/shard_map/template_planes/pallas_call | solution.py:370
  40.8 0.0 copy-done.1
  40.8 1.9 %factors.5 = (f32[8,3,48,128]{3,2,1,0:T(8,128)S(1)}, f32[8,128]{1,0:T(8,128)S(1)}) custom-call(s32[6]{0:T(128)S(1)} %stack.27.idx, f32[4,104,48,128]{3,2,1,0:T(8,128)S(1)} %get-tuple-element.27.iplane, f32[4,104,48,128]{3,2,1,0:T(8,128)S(1)} %copy-done.1, f32[3,96,56,128]{3,2,1,0:T(8,128)S(1)} %get-tuple-element.29.raw), custom_call_target="tpu_custom_call" | custom-call | flops 400000000 | bytes 1000000 | tf_op jit(solution)/shard_map/factors/pallas_call | solution.py:431
  42.7 0.9 collective-permute-start.1
  43.5 1.8 %factors.6 = (f32[8,3,48,128]{3,2,1,0:T(8,128)S(1)}, f32[8,128]{1,0:T(8,128)S(1)}) custom-call(s32[6]{0:T(128)S(1)} %stack.27.idx, f32[4,104,48,128]{3,2,1,0:T(8,128)S(1)} %get-tuple-element.27.iplane, f32[4,104,48,128]{3,2,1,0:T(8,128)S(1)} %copy-done.1, f32[3,96,56,128]{3,2,1,0:T(8,128)S(1)} %get-tuple-element.29.raw), custom_call_target="tpu_custom_call" | custom-call | flops 400000000 | bytes 1000000 | tf_op jit(solution)/shard_map/factors/pallas_call | solution.py:431
  45.4 2.0 %collective-permute-start.2 = (f32[8,3,48,128]{3,2,1,0:T(8,128)S(1)}, f32[8,3,48,128]{3,2,1,0:T(8,128)S(1)}, u32[]{:S(2)}, u32[]{:S(2)}) collective-permute-start(f32[8,3,48,128]{3,2,1,0:T(8,128)S(1)} %get-tuple-element.32), channel_id=1, source_target_pairs={{0,2},{1,3},{2,0},{3,1},{4,6},{5,7},{6,4},{7,5},{8,10},{9,11},{10,... | collective-permute-start | bytes 1769480 | tf_op jit(solution)/shard_map/ppermute | solution.py:76
  47.4 1.8 %factors.7 = (f32[8,3,48,128]{3,2,1,0:T(8,128)S(1)}, f32[8,128]{1,0:T(8,128)S(1)}) custom-call(s32[6]{0:T(128)S(1)} %stack.27.idx, f32[4,104,48,128]{3,2,1,0:T(8,128)S(1)} %get-tuple-element.27.iplane, f32[4,104,48,128]{3,2,1,0:T(8,128)S(1)} %copy-done.1, f32[3,96,56,128]{3,2,1,0:T(8,128)S(1)} %get-tuple-element.29.raw), custom_call_target="tpu_custom_call" | custom-call | flops 400000000 | bytes 1000000 | tf_op jit(solution)/shard_map/factors/pallas_call | solution.py:431
  49.1 0.0 collective-permute-done.4
  49.1 0.0 copy-start.2
  49.2 1.8 %collective-permute-start.3 = (f32[8,3,48,128]{3,2,1,0:T(8,128)S(1)}, f32[8,3,48,128]{3,2,1,0:T(8,128)S(1)}, u32[]{:S(2)}, u32[]{:S(2)}) collective-permute-start(f32[8,3,48,128]{3,2,1,0:T(8,128)S(1)} %get-tuple-element.33), channel_id=1, source_target_pairs={{0,3},{1,0},{2,1},{3,2},{4,7},{5,4},{6,5},{7,6},{8,11},{9,8},{10,9... | collective-permute-start | bytes 1769480 | tf_op jit(solution)/shard_map/ppermute | solution.py:76
  50.9 1.8 %factors.4 = (f32[8,3,48,128]{3,2,1,0:T(8,128)S(1)}, f32[8,128]{1,0:T(8,128)S(1)}) custom-call(s32[6]{0:T(128)S(1)} %stack.27.idx, f32[4,104,48,128]{3,2,1,0:T(8,128)S(1)} %get-tuple-element.27.iplane, f32[4,104,48,128]{3,2,1,0:T(8,128)S(1)} %copy-done.1, f32[3,96,56,128]{3,2,1,0:T(8,128)S(1)} %get-tuple-element.29.raw), custom_call_target="tpu_custom_call" | custom-call | flops 400000000 | bytes 1000000 | tf_op jit(solution)/shard_map/factors/pallas_call | solution.py:431
  52.8 0.0 collective-permute-done.5
  52.8 0.0 collective-permute-done.6
  52.8 0.0 copy-done.2
  52.8 0.1 add_add_fusion
  53.0 7.2 %collective-permute-done.1 = f32[8,3,48,128]{3,2,1,0:T(8,128)S(1)} collective-permute-done((f32[8,3,48,128]{3,2,1,0:T(8,128)S(1)}, f32[8,3,48,128]{3,2,1,0:T(8,128)S(1)}, u32[]{:S(2)}, u32[]{:S(2)}) %collective-permute-start.1) | collective-permute-done | bytes 589856 | tf_op jit(solution)/shard_map/ppermute | solution.py:76
  60.1 0.0 collective-permute-done.2
  60.1 2.8 %collective-permute-done.3 = f32[8,3,48,128]{3,2,1,0:T(8,128)S(1)} collective-permute-done((f32[8,3,48,128]{3,2,1,0:T(8,128)S(1)}, f32[8,3,48,128]{3,2,1,0:T(8,128)S(1)}, u32[]{:S(2)}, u32[]{:S(2)}) %collective-permute-start.3) | collective-permute-done | bytes 589856 | tf_op jit(solution)/shard_map/ppermute | solution.py:76
  63.0 0.2 add_add_fusion.1
  63.1 0.1 fusion.5
  63.2 3.4 %collective-permute-start.7 = (f32[2,6,48,128]{3,2,1,0:T(8,128)S(1)}, f32[2,6,48,128]{3,2,1,0:T(8,128)S(1)}, u32[]{:S(2)}, u32[]{:S(2)}) collective-permute-start(f32[2,6,48,128]{3,2,1,0:T(8,128)S(1)} %get-tuple-element.51), channel_id=1, source_target_pairs={{0,8},{1,9},{2,10},{3,11},{4,12},{5,13},{6,14},{7,15},{8,0},{9,1},... | collective-permute-start | bytes 884744 | tf_op jit(solution)/shard_map/ppermute | solution.py:76
  66.6 0.0 collective-permute-start.8
  66.6 3.2 %collective-permute-start.9 = (f32[2,6,48,128]{3,2,1,0:T(8,128)S(1)}, f32[2,6,48,128]{3,2,1,0:T(8,128)S(1)}, u32[]{:S(2)}, u32[]{:S(2)}) collective-permute-start(f32[2,6,48,128]{3,2,1,0:T(8,128)S(1)} %get-tuple-element.52), channel_id=1, source_target_pairs={{0,12},{1,13},{2,14},{3,15},{4,0},{5,1},{6,2},{7,3},{8,4},{9,5},{1... | collective-permute-start | bytes 884744 | tf_op jit(solution)/shard_map/ppermute | solution.py:76
  69.8 1.7 %collective-permute-done.7 = f32[2,6,48,128]{3,2,1,0:T(8,128)S(1)} collective-permute-done((f32[2,6,48,128]{3,2,1,0:T(8,128)S(1)}, f32[2,6,48,128]{3,2,1,0:T(8,128)S(1)}, u32[]{:S(2)}, u32[]{:S(2)}) %collective-permute-start.7) | collective-permute-done | bytes 294944 | tf_op jit(solution)/shard_map/ppermute | solution.py:76
  71.5 3.1 %collective-permute-done.8 = f32[2,6,48,128]{3,2,1,0:T(8,128)S(1)} collective-permute-done((f32[2,6,48,128]{3,2,1,0:T(8,128)S(1)}, f32[2,6,48,128]{3,2,1,0:T(8,128)S(1)}, u32[]{:S(2)}, u32[]{:S(2)}) %collective-permute-start.8) | collective-permute-done | bytes 294944 | tf_op jit(solution)/shard_map/ppermute | solution.py:76
  74.7 0.0 collective-permute-done.9
  74.7 0.1 fusion.4
  74.8 2.8 %collective-permute-start.10 = (f32[296,128]{1,0:T(8,128)S(1)}, f32[296,128]{1,0:T(8,128)S(1)}, u32[]{:S(2)}, u32[]{:S(2)}) collective-permute-start(f32[296,128]{1,0:T(8,128)S(1)} %get-tuple-element.54), channel_id=1, source_target_pairs={{0,64},{1,65},{2,66},{3,67},{4,68},{5,69},{6,70},{7,71},{8,72},{9,... | collective-permute-start | bytes 454664 | tf_op jit(solution)/shard_map/ppermute | solution.py:76
  77.6 0.2 collective-permute-start.11
  77.8 3.1 %collective-permute-start.12 = (f32[296,128]{1,0:T(8,128)S(1)}, f32[296,128]{1,0:T(8,128)S(1)}, u32[]{:S(2)}, u32[]{:S(2)}) collective-permute-start(f32[296,128]{1,0:T(8,128)S(1)} %get-tuple-element.55), channel_id=1, source_target_pairs={{0,80},{1,81},{2,82},{3,83},{4,84},{5,85},{6,86},{7,87},{8,88},{9,... | collective-permute-start | bytes 454664 | tf_op jit(solution)/shard_map/ppermute | solution.py:76
  80.8 0.7 collective-permute-done.10
  81.6 2.4 %collective-permute-done.11 = f32[296,128]{1,0:T(8,128)S(1)} collective-permute-done((f32[296,128]{1,0:T(8,128)S(1)}, f32[296,128]{1,0:T(8,128)S(1)}, u32[]{:S(2)}, u32[]{:S(2)}) %collective-permute-start.11) | collective-permute-done | bytes 151584 | tf_op jit(solution)/shard_map/ppermute | solution.py:76
  84.0 0.0 collective-permute-done.12
  84.1 1.1 collective-permute-start.14
  85.2 3.0 %collective-permute-start.13 = (f32[96,128]{1,0:T(8,128)S(1)}, f32[96,128]{1,0:T(8,128)S(1)}, u32[]{:S(2)}, u32[]{:S(2)}) collective-permute-start(f32[96,128]{1,0:T(8,128)S(1)} %slice_select_fusion), channel_id=1, source_target_pairs={{0,2},{1,3},{2,4},{3,5},{4,6},{5,7},{6,8},{7,9},{8,10},{9,11},{10,... | collective-permute-start | bytes 147464 | tf_op jit(solution)/shard_map/ppermute | solution.py:76
  88.3 5.0 %collective-permute-done.14 = f32[192,128]{1,0:T(8,128)S(1)} collective-permute-done((f32[192,128]{1,0:T(8,128)S(1)}, f32[192,128]{1,0:T(8,128)S(1)}, u32[]{:S(2)}, u32[]{:S(2)}) %collective-permute-start.14) | collective-permute-done | bytes 98336 | tf_op jit(solution)/shard_map/ppermute | solution.py:76
  93.3 0.9 collective-permute-done.13
  94.2 4.8 %collective-permute-start.15 = (f32[288,128]{1,0:T(8,128)S(1)}, f32[288,128]{1,0:T(8,128)S(1)}, u32[]{:S(2)}, u32[]{:S(2)}) collective-permute-start(f32[288,128]{1,0:T(8,128)S(1)} %pad_maximum_fusion.4), channel_id=1, source_target_pairs={{0,64},{1,65},{2,66},{3,67},{4,68},{5,69},{6,70},{7,71},{8,72},{9,... | collective-permute-start | bytes 442376 | tf_op jit(solution)/shard_map/ppermute | solution.py:76
  99.1 3.1 %collective-permute-done.15.twin_ref = f32[288,128]{1,0:T(8,128)S(1)} collective-permute-done((f32[288,128]{1,0:T(8,128)S(1)}, f32[288,128]{1,0:T(8,128)S(1)}, u32[]{:S(2)}, u32[]{:S(2)}) %collective-permute-start.15) | collective-permute-done | bytes 147488 | tf_op jit(solution)/shard_map/ppermute | solution.py:76
  102.2 0.1 collective-permute-start.16
  102.3 0.5 collective-permute-start.17
  102.8 1.6 %collective-permute-done.17.iother_ref = bf16[15,48,128]{2,1,0:T(8,128)(2,1)S(1)} collective-permute-done((bf16[15,48,128]{2,1,0:T(8,128)(2,1)S(1)}, bf16[15,48,128]{2,1,0:T(8,128)(2,1)S(1)}, u32[]{:S(2)}, u32[]{:S(2)}) %collective-permute-start.17) | collective-permute-done | bytes 184352 | tf_op jit(solution)/shard_map/ppermute | solution.py:76
  104.4 1.0 slopes.1.slope_ref
  105.4 0.0 collective-permute-done.16.other_ref
  105.4 2.6 %smooth_slab.1 = (f32[3,3,96,128]{3,2,1,0:T(8,128)S(1)}, f32[3,96,128]{2,1,0:T(8,128)S(1)}, f32[3,96,128]{2,1,0:T(8,128)S(1)}, f32[1,128]{1,0:T(1,128)S(1)}) custom-call(s32[6]{0:T(128)S(1)} %stack.27.idx, f32[584,128]{1,0:T(8,128)S(1)} %pad_maximum_fusion.1.own_ref, f32[288,128]{1,0:T(8,128)S(1)} %collective-permute-done.15.twin_ref, ...), custom_call_target="tpu_custom_call" | custom-call | flops 100000000 | bytes 3000000 | tf_op jit(solution)/shard_map/smooth_slab/pallas_call | solution.py:579
  108.1 13.2 %all_to_all.10 = f32[32,1,128]{2,1,0:T(1,128)S(1)} all-to-all(f32[32,1,128]{2,1,0:T(1,128)S(1)} %broadcast_in_dim.11), channel_id=1, replica_groups=mesh['grp'=4,'sub'=32] {'sub'}, dimensions={0} | all-to-all | bytes 32768 | tf_op jit(solution)/shard_map/all_to_all | solution.py:702
  121.3 0.9 finish.1
  (16 shorter events, 0.2 us)
Async XLA Ops:
  0.6 0.9 copy-start
  0.6 11.7 %collective-permute-start = (bf16[96,96,128]{2,1,0:T(8,128)(2,1)}, bf16[96,96,128]{2,1,0:T(8,128)(2,1)}, u32[]{:S(2)}, u32[]{:S(2)}) collective-permute-start(bf16[96,96,128]{2,1,0:T(8,128)(2,1)} %bitcast.23), channel_id=1, source_target_pairs={{0,32},{1,33},{2,34},{3,35},{4,36},{5,37},{6,38},{7,39},{8,40},{9,... | collective-permute-start | bytes 7077896 | tf_op jit(solution)/shard_map/ppermute | solution.py:76
  2.8 29.9 %all-to-all-start = ((bf16[32,3,56,128]{3,2,1,0:T(8,128)(2,1)}), bf16[32,3,56,128]{3,2,1,0:T(8,128)(2,1)S(1)}, u32[]{:S(2)}, u32[]{:S(2)}) async-start(bf16[32,3,56,128]{3,2,1,0:T(8,128)(2,1)} %broadcast_in_dim.8), calls=%async_computation | async-start | bytes 2752512 | tf_op jit(solution)/shard_map/all_to_all | solution.py:660
  22.0 27.1 %collective-permute-start.4 = (f32[8,3,48,128]{3,2,1,0:T(8,128)}, f32[8,3,48,128]{3,2,1,0:T(8,128)S(1)}, u32[]{:S(2)}, u32[]{:S(2)}) collective-permute-start(f32[8,3,48,128]{3,2,1,0:T(8,128)} %get-tuple-element.40), channel_id=1, source_target_pairs={{0,1},{1,2},{2,3},{3,0},{4,5},{5,6},{6,7},{7,4},{8,9},{9,10},{10,1... | collective-permute-start | bytes 1769480 | tf_op jit(solution)/shard_map/ppermute | solution.py:76
  23.8 28.9 %collective-permute-start.5 = (f32[8,3,48,128]{3,2,1,0:T(8,128)}, f32[8,3,48,128]{3,2,1,0:T(8,128)S(1)}, u32[]{:S(2)}, u32[]{:S(2)}) collective-permute-start(f32[8,3,48,128]{3,2,1,0:T(8,128)} %get-tuple-element.41), channel_id=1, source_target_pairs={{0,3},{1,0},{2,1},{3,2},{4,7},{5,4},{6,5},{7,6},{8,11},{9,8},{10,9... | collective-permute-start | bytes 1769480 | tf_op jit(solution)/shard_map/ppermute | solution.py:76
  25.3 27.5 %collective-permute-start.6 = (f32[8,3,48,128]{3,2,1,0:T(8,128)}, f32[8,3,48,128]{3,2,1,0:T(8,128)S(1)}, u32[]{:S(2)}, u32[]{:S(2)}) collective-permute-start(f32[8,3,48,128]{3,2,1,0:T(8,128)} %get-tuple-element.42), channel_id=1, source_target_pairs={{0,2},{1,3},{2,0},{3,1},{4,6},{5,7},{6,4},{7,5},{8,10},{9,11},{10,... | collective-permute-start | bytes 1769480 | tf_op jit(solution)/shard_map/ppermute | solution.py:76
  32.7 8.1 %copy-start.1 = (f32[4,104,48,128]{3,2,1,0:T(8,128)S(1)}, f32[4,104,48,128]{3,2,1,0:T(8,128)}, u32[]{:S(2)}) copy-start(f32[4,104,48,128]{3,2,1,0:T(8,128)} %get-tuple-element.28.jplane) | copy-start | bytes 30670852
  42.7 17.5 %collective-permute-start.1 = (f32[8,3,48,128]{3,2,1,0:T(8,128)S(1)}, f32[8,3,48,128]{3,2,1,0:T(8,128)S(1)}, u32[]{:S(2)}, u32[]{:S(2)}) collective-permute-start(f32[8,3,48,128]{3,2,1,0:T(8,128)S(1)} %get-tuple-element.31), channel_id=1, source_target_pairs={{0,1},{1,2},{2,3},{3,0},{4,5},{5,6},{6,7},{7,4},{8,9},{9,10},{10,1... | collective-permute-start | bytes 1769480 | tf_op jit(solution)/shard_map/ppermute | solution.py:76
  45.4 14.8 %collective-permute-start.2 = (f32[8,3,48,128]{3,2,1,0:T(8,128)S(1)}, f32[8,3,48,128]{3,2,1,0:T(8,128)S(1)}, u32[]{:S(2)}, u32[]{:S(2)}) collective-permute-start(f32[8,3,48,128]{3,2,1,0:T(8,128)S(1)} %get-tuple-element.32), channel_id=1, source_target_pairs={{0,2},{1,3},{2,0},{3,1},{4,6},{5,7},{6,4},{7,5},{8,10},{9,11},{10,... | collective-permute-start | bytes 1769480 | tf_op jit(solution)/shard_map/ppermute | solution.py:76
  49.1 3.7 %copy-start.2 = (f32[8,3,48,128]{3,2,1,0:T(8,128)S(1)}, f32[8,3,48,128]{3,2,1,0:T(8,128)}, u32[]{:S(2)}) copy-start(f32[8,3,48,128]{3,2,1,0:T(8,128)} %get-tuple-element.39) | copy-start | bytes 1769476
  49.2 13.8 %collective-permute-start.3 = (f32[8,3,48,128]{3,2,1,0:T(8,128)S(1)}, f32[8,3,48,128]{3,2,1,0:T(8,128)S(1)}, u32[]{:S(2)}, u32[]{:S(2)}) collective-permute-start(f32[8,3,48,128]{3,2,1,0:T(8,128)S(1)} %get-tuple-element.33), channel_id=1, source_target_pairs={{0,3},{1,0},{2,1},{3,2},{4,7},{5,4},{6,5},{7,6},{8,11},{9,8},{10,9... | collective-permute-start | bytes 1769480 | tf_op jit(solution)/shard_map/ppermute | solution.py:76
  63.2 8.3 %collective-permute-start.7 = (f32[2,6,48,128]{3,2,1,0:T(8,128)S(1)}, f32[2,6,48,128]{3,2,1,0:T(8,128)S(1)}, u32[]{:S(2)}, u32[]{:S(2)}) collective-permute-start(f32[2,6,48,128]{3,2,1,0:T(8,128)S(1)} %get-tuple-element.51), channel_id=1, source_target_pairs={{0,8},{1,9},{2,10},{3,11},{4,12},{5,13},{6,14},{7,15},{8,0},{9,1},... | collective-permute-start | bytes 884744 | tf_op jit(solution)/shard_map/ppermute | solution.py:76
  66.6 8.1 %collective-permute-start.8 = (f32[2,6,48,128]{3,2,1,0:T(8,128)S(1)}, f32[2,6,48,128]{3,2,1,0:T(8,128)S(1)}, u32[]{:S(2)}, u32[]{:S(2)}) collective-permute-start(f32[2,6,48,128]{3,2,1,0:T(8,128)S(1)} %get-tuple-element.53), channel_id=1, source_target_pairs={{0,4},{1,5},{2,6},{3,7},{4,8},{5,9},{6,10},{7,11},{8,12},{9,13},{1... | collective-permute-start | bytes 884744 | tf_op jit(solution)/shard_map/ppermute | solution.py:76
  66.6 8.1 %collective-permute-start.9 = (f32[2,6,48,128]{3,2,1,0:T(8,128)S(1)}, f32[2,6,48,128]{3,2,1,0:T(8,128)S(1)}, u32[]{:S(2)}, u32[]{:S(2)}) collective-permute-start(f32[2,6,48,128]{3,2,1,0:T(8,128)S(1)} %get-tuple-element.52), channel_id=1, source_target_pairs={{0,12},{1,13},{2,14},{3,15},{4,0},{5,1},{6,2},{7,3},{8,4},{9,5},{1... | collective-permute-start | bytes 884744 | tf_op jit(solution)/shard_map/ppermute | solution.py:76
  74.8 6.8 %collective-permute-start.10 = (f32[296,128]{1,0:T(8,128)S(1)}, f32[296,128]{1,0:T(8,128)S(1)}, u32[]{:S(2)}, u32[]{:S(2)}) collective-permute-start(f32[296,128]{1,0:T(8,128)S(1)} %get-tuple-element.54), channel_id=1, source_target_pairs={{0,64},{1,65},{2,66},{3,67},{4,68},{5,69},{6,70},{7,71},{8,72},{9,... | collective-permute-start | bytes 454664 | tf_op jit(solution)/shard_map/ppermute | solution.py:76
  77.6 6.4 %collective-permute-start.11 = (f32[296,128]{1,0:T(8,128)S(1)}, f32[296,128]{1,0:T(8,128)S(1)}, u32[]{:S(2)}, u32[]{:S(2)}) collective-permute-start(f32[296,128]{1,0:T(8,128)S(1)} %get-tuple-element.55), channel_id=1, source_target_pairs={{0,16},{1,17},{2,18},{3,19},{4,20},{5,21},{6,22},{7,23},{8,24},{9,... | collective-permute-start | bytes 454664 | tf_op jit(solution)/shard_map/ppermute | solution.py:76
  77.8 6.2 %collective-permute-start.12 = (f32[296,128]{1,0:T(8,128)S(1)}, f32[296,128]{1,0:T(8,128)S(1)}, u32[]{:S(2)}, u32[]{:S(2)}) collective-permute-start(f32[296,128]{1,0:T(8,128)S(1)} %get-tuple-element.55), channel_id=1, source_target_pairs={{0,80},{1,81},{2,82},{3,83},{4,84},{5,85},{6,86},{7,87},{8,88},{9,... | collective-permute-start | bytes 454664 | tf_op jit(solution)/shard_map/ppermute | solution.py:76
  84.1 9.2 %collective-permute-start.14 = (f32[192,128]{1,0:T(8,128)S(1)}, f32[192,128]{1,0:T(8,128)S(1)}, u32[]{:S(2)}, u32[]{:S(2)}) collective-permute-start(f32[192,128]{1,0:T(8,128)S(1)} %pad_maximum_fusion.5), channel_id=1, source_target_pairs={{0,1},{1,2},{2,3},{3,4},{4,5},{5,6},{6,7},{7,8},{8,9},{9,10},{10,1... | collective-permute-start | bytes 294920 | tf_op jit(solution)/shard_map/ppermute | solution.py:76
  85.2 9.0 %collective-permute-start.13 = (f32[96,128]{1,0:T(8,128)S(1)}, f32[96,128]{1,0:T(8,128)S(1)}, u32[]{:S(2)}, u32[]{:S(2)}) collective-permute-start(f32[96,128]{1,0:T(8,128)S(1)} %slice_select_fusion), channel_id=1, source_target_pairs={{0,2},{1,3},{2,4},{3,5},{4,6},{5,7},{6,8},{7,9},{8,10},{9,11},{10,... | collective-permute-start | bytes 147464 | tf_op jit(solution)/shard_map/ppermute | solution.py:76
  94.2 8.0 %collective-permute-start.15 = (f32[288,128]{1,0:T(8,128)S(1)}, f32[288,128]{1,0:T(8,128)S(1)}, u32[]{:S(2)}, u32[]{:S(2)}) collective-permute-start(f32[288,128]{1,0:T(8,128)S(1)} %pad_maximum_fusion.4), channel_id=1, source_target_pairs={{0,64},{1,65},{2,66},{3,67},{4,68},{5,69},{6,70},{7,71},{8,72},{9,... | collective-permute-start | bytes 442376 | tf_op jit(solution)/shard_map/ppermute | solution.py:76
  102.2 3.2 %collective-permute-start.16 = (f32[872,128]{1,0:T(8,128)S(1)}, f32[872,128]{1,0:T(8,128)S(1)}, u32[]{:S(2)}, u32[]{:S(2)}) collective-permute-start(f32[872,128]{1,0:T(8,128)S(1)} %pad_maximum_fusion), channel_id=1, source_target_pairs={{0,32},{1,33},{2,34},{3,35},{4,36},{5,37},{6,38},{7,39},{8,40},{9,... | collective-permute-start | bytes 1339400 | tf_op jit(solution)/shard_map/ppermute | solution.py:76
  102.3 2.0 %collective-permute-start.17 = (bf16[15,48,128]{2,1,0:T(8,128)(2,1)S(1)}, bf16[15,48,128]{2,1,0:T(8,128)(2,1)S(1)}, u32[]{:S(2)}, u32[]{:S(2)}) collective-permute-start(bf16[15,48,128]{2,1,0:T(8,128)(2,1)S(1)} %get-tuple-element.43.iown_ref), channel_id=1, source_target_pairs={{0,32},{1,33},{2,34},{3,35},{4,36},{5,37},{6,38},{7,39},{8,40},{9,... | collective-permute-start | bytes 552968 | tf_op jit(solution)/shard_map/ppermute | solution.py:76
